TPU v7x, 256 devices: a whole 4x4x8 slice. The times are simulated.
256 devices in a mesh: grp: 8 (over y, core), seq: 32 (over x, z).
Axes of the slice: x: 4, y: 4, z: 8, core: 2. Of those that a mesh axis runs over, the one named last changes fastest.
Arguments:
- query: bfloat16 [131072, 1024], P(('grp', 'seq')), may hold values from -6 to 6
- key_in: bfloat16 [131072, 1024], P(('grp', 'seq')), may hold values from -6 to 6
- value: bfloat16 [131072, 1024], P(('grp', 'seq')), may hold values from -6 to 6
- gate: bfloat16 [131072, 1024], P(('grp', 'seq')), may hold values from -6 to 6
- gain: float32 [1024], replicated, may hold values from 0.1 to 1.9
Outputs:
- attended: bfloat16 [131072, 1024], P(('grp', 'seq'))
All inputs are finite; a program needn't handle non-finite values.
Results may differ from a plain program's by a relative error of at most 0.0046.
Values sent between devices are 32-bit elements; how exact they have to be, the bound alone decides.
No kernel may reach another device: no remote copies, remote signals or barrier semaphores. Data moves between devices by JAX's collectives and lax.ppermute only.
A program may use at most 320 MiB of HBM per device.

v0:
```python
import jax
import jax.numpy as jnp
from jax import lax
from jax.sharding import PartitionSpec as P

HEADS = 8
HEAD_DIM = 128
BLOCK = 256


def prefix(part, axis, combine, identity):
    place = lax.axis_index(axis)
    gathered = lax.all_gather(part, axis)
    state = jnp.zeros_like(part) + jnp.asarray(identity, part.dtype)

    def one(step, state):
        return combine(state, lax.dynamic_index_in_dim(gathered, step, 0, False))

    return lax.fori_loop(0, place, one, state)


def per_device(query, key_in, value, gate, gain):
    rows_here = query.shape[0]
    count = rows_here // BLOCK
    queries = jax.nn.silu(query.astype(jnp.float32)).astype(jnp.bfloat16)
    keys_act = jax.nn.silu(key_in.astype(jnp.float32)).astype(jnp.bfloat16)
    queries = queries.reshape(count, BLOCK, HEADS, HEAD_DIM)
    keys_act = keys_act.reshape(count, BLOCK, HEADS, HEAD_DIM)
    values_in = value.reshape(count, BLOCK, HEADS, HEAD_DIM)
    block_kv = jnp.einsum(
        "bthd,bthe->bhde", keys_act, values_in, preferred_element_type=jnp.float32
    )
    own_total = jnp.sum(block_kv, axis=0)
    nothing = jnp.zeros_like(own_total)
    within = prefix(own_total, "seq", jnp.add, nothing)
    range_total = lax.psum(own_total, "seq")
    before = prefix(range_total, "grp", jnp.add, nothing)
    carried = before + within
    earlier = jnp.cumsum(block_kv, axis=0) - block_kv + carried[None]
    causal = jnp.arange(BLOCK)[:, None] >= jnp.arange(BLOCK)[None, :]
    scores = jnp.einsum("bthd,bshd->bhts", queries, keys_act, preferred_element_type=jnp.float32)
    scores = jnp.where(causal[None, None], scores, 0.0).astype(jnp.bfloat16)
    inner = jnp.einsum("bhts,bshd->bthd", scores, values_in, preferred_element_type=jnp.float32)
    outer = jnp.einsum(
        "bthd,bhde->bthe", queries.astype(jnp.float32), earlier, precision=lax.Precision.HIGHEST
    )
    mixed = (inner + outer).reshape(rows_here, HEADS, HEAD_DIM)
    power = jnp.mean(mixed * mixed, axis=-1, keepdims=True)
    normed = (mixed / jnp.sqrt(power + 1e-05)).reshape(rows_here, HEADS * HEAD_DIM)
    result = normed * gain[None, :] * jax.nn.sigmoid(gate.astype(jnp.float32))
    return result.astype(jnp.bfloat16)


def solution(mesh):
    return jax.shard_map(
        per_device,
        mesh=mesh,
        in_specs=(
            P(("grp", "seq"), None),
            P(("grp", "seq"), None),
            P(("grp", "seq"), None),
            P(("grp", "seq"), None),
            P(),
        ),
        out_specs=P(("grp", "seq"), None),
        check_vma=False,
    )
```

profile of v0, /device:TPU:254, one launch (start us, length us, event | category | flops | bytes accessed | tf_op | source)
XLA Modules:
  0.0 366.0 jit_solution(9238966633678830877)
XLA Ops:
  6.5 1.8 fusion.13
  9.3 1.5 copy.37
  10.8 1.2 fusion.22
  12.0 136.9 %all-gather.6.cloned.1.call-done = f32[256,128,128]{2,1,0:T(8,128)} async-done(((f32[8,128,128]{2,1,0:T(8,128)}), f32[256,128,128]{2,1,0:T(8,128)}) %all-gather.6.cloned.1.call-update) | async-done | bytes 16777232 | tf_op jit(solution)/shard_map/all_gather | solution.py:13
  149.8 149.1 %all-reduce.2.cloned.1.call-done = f32[1,8,128,128]{3,2,1,0:T(8,128)} async-done(((f32[1,8,128,128]{3,2,1,0:T(8,128)}), f32[1,8,128,128]{3,2,1,0:T(8,128)}) %all-reduce.2.cloned.1.call-update) | async-done | bytes 524304 | tf_op jit(solution)/shard_map/psum | solution.py:36
  298.9 1.8 fusion.14
  300.7 1.2 copy.35
  302.0 3.9 %fusion.11 = f32[2,8,256,128]{2,3,1,0:T(8,128)} fusion(bf16[2,256,8,128]{1,3,2,0:T(8,128)(2,1)S(1)} %copy.28, pred[256,256]{1,0:T(8,128)(4,1)S(1)} %iota_compare_fusion, bf16[2,256,8,128]{3,2,1,0:T(8,128)(2,1)S(1)} %bitcast.47, bf16[2,256,8,128]{3,2,1,0:T(8,128)(2,1)} %bitcast.49), kind=kOutput, calls=%fused_computation.21 | convolution fusion | flops 538968064 | bytes 5308416 | tf_op jit(solution)/shard_map/bhts,bshd->bthd/dot_general | solution.py:43
  305.9 37.2 %while.21 = (s32[]{:T(128)}, f32[8,128,128]{2,1,0:T(8,128)S(1)}, s32[]{:T(128)}, f32[32,8,128,128]{3,2,1,0:T(8,128)}, s32[]{:T(128)}, /*index=5*/s32[]{:T(128)}, s32[]{:T(128)}) while((s32[]{:T(128)}, f32[8,128,128]{2,1,0:T(8,128)S(1)}, s32[]{:T(128)}, f32[32,8,128,128]{3,2,1,0:T(8,128)}, s32[]{:T(128)}, /*index=5*/s32[]{:T(128)}, ...), condition=%wide.region_6.7_spmd, body=%wide.region_5.6_spmd.sunk | while | flops 131077 | bytes 1572987 | solution.py:19
  308.3 1.2 bitcast_add_fusion.6
  310.7 1.2 bitcast_add_fusion.6
  311.9 1.2 bitcast_add_fusion.6
  313.1 1.3 bitcast_add_fusion.6
  314.4 1.2 bitcast_add_fusion.6
  316.8 1.2 bitcast_add_fusion.6
  319.2 1.2 bitcast_add_fusion.6
  321.6 1.2 bitcast_add_fusion.6
  322.8 1.2 bitcast_add_fusion.6
  324.0 1.2 bitcast_add_fusion.6
  325.2 1.2 bitcast_add_fusion.6
  343.2 7.2 %while.20 = (s32[]{:T(128)}, f32[8,128,128]{2,1,0:T(8,128)S(1)}, s32[]{:T(128)}, f32[8,8,128,128]{3,2,1,0:T(8,128)}, s32[]{:T(128)}, /*index=5*/s32[]{:T(128)}, s32[]{:T(128)}) while((s32[]{:T(128)}, f32[8,128,128]{2,1,0:T(8,128)S(1)}, s32[]{:T(128)}, f32[8,8,128,128]{3,2,1,0:T(8,128)}, s32[]{:T(128)}, /*index=5*/s32[]{:T(128)}, ...), condition=%wide.region_4.5_spmd, body=%wide.region_3.4_spmd.sunk | while | flops 131077 | bytes 1572987 | solution.py:19
  352.3 1.3 multiply_reduce_fusion
  353.8 1.9 copy.32
  357.2 2.2 fusion.10
  (53 shorter events, 35.9 us)
Async XLA Ops:
  6.5 142.5 %all-gather.6.cloned.1.call-start = ((), (), s32[]{:S(2)}) async-start(), calls=%async_computation.2 | async-start | bytes 17301504 | tf_op jit(solution)/shard_map/all_gather | solution.py:13
  149.0 149.9 %all-reduce.2.cloned.1.call-start = ((), (), s32[]{:S(2)}) async-start(), calls=%async_computation | async-start | bytes 1048576 | tf_op jit(solution)/shard_map/psum | solution.py:36
  149.7 193.4 %all-gather.4.cloned.1.call-start = ((), (), s32[]{:S(2)}) async-start(), calls=%async_computation.1 | async-start | bytes 4718592 | tf_op jit(solution)/shard_map/all_gather | solution.py:13
  350.4 1.2 copy-start.1
  350.4 1.9 copy-start.2
  353.7 2.5 copy-start.3
  355.7 1.6 copy-start
  355.7 1.6 copy-start.4
Sparse Core Ops, SparseCore 0:
  12.2 136.7 all-gather.5
  153.2 145.6 all-reduce.1
  300.9 32.3 all-gather.3
where the time goes:
time: 368 us; the launch traced here: 366 us
  waiting for transfers between devices  287 us (78%)
  other arithmetic  49.7 us (14%)
  between operations  13.2 us (4%)
  local copies, waits for them, and re-layouts  8.98 us (2%)
  matrix products  6.38 us (2%)
    psum x1, waiting for transfers between devices, per_device(): range_total = lax.psum(own_total, 'seq')  149 us
    all_gather x2, waiting for transfers between devices, prefix(): gathered = lax.all_gather(part, axis)  137 us
    add x37, other arithmetic, one(): return combine(state, lax.dynamic_index_in_dim(gathered, step, 0, False))  43.5 us
  transfers between devices with their start and end apart: 3, of which 2 were waited for; matrix products, arithmetic and copies ran while one was open for 12% of the time, Pallas kernels for 0%

commit v1 on v0

v1 whole, which is shorter than its diff:
```python
import functools

import jax
import jax.numpy as jnp
from jax import lax
from jax.experimental import pallas as pl
from jax.experimental.pallas import tpu as pltpu
from jax.sharding import PartitionSpec as P

HEADS = 8
HEAD_DIM = 128
BLOCK = 256
LANES = 2 * HEAD_DIM
VMEM_LIMIT = 48 * 1024 * 1024


def silu(u):
    u = u.astype(jnp.float32)
    return (u / (1.0 + jnp.exp(-u))).astype(jnp.bfloat16)


def dot(a, b, contract):
    return lax.dot_general(a, b, ((contract[0], contract[1]), ((), ())), preferred_element_type=jnp.float32)


def wide_dot(a, state):
    high = state.astype(jnp.bfloat16)
    low = (state - high.astype(jnp.float32)).astype(jnp.bfloat16)
    return dot(jnp.concatenate([a, a], axis=1), jnp.concatenate([high, low], axis=0), ((1,), (0,)))


def kv_body(key_ref, value_ref, keys_ref, first_ref, total_ref):
    count = key_ref.shape[0] // BLOCK
    for b in range(count):
        rows = pl.ds(b * BLOCK, BLOCK)
        keys = silu(key_ref[rows, :])
        keys_ref[rows, :] = keys
        for h in range(LANES // HEAD_DIM):
            cols = slice(h * HEAD_DIM, (h + 1) * HEAD_DIM)
            state = dot(keys[:, cols], value_ref[rows, cols], ((0,), (0,)))
            out = slice(h * HEAD_DIM, (h + 1) * HEAD_DIM)
            if b == 0:
                first_ref[out, :] = state
                total_ref[out, :] = state
            else:
                total_ref[out, :] = total_ref[out, :] + state


def intra_body(query_ref, keys_ref, value_ref, gate_ref, gain_ref, first_ref, queries_ref, inner_ref, scale_ref):
    row = lax.broadcasted_iota(jnp.int32, (BLOCK, BLOCK), 0)
    col = lax.broadcasted_iota(jnp.int32, (BLOCK, BLOCK), 1)
    causal = row >= col
    for b in range(query_ref.shape[0] // BLOCK):
        rows = pl.ds(b * BLOCK, BLOCK)
        queries = silu(query_ref[rows, :])
        queries_ref[rows, :] = queries
        gate = gate_ref[rows, :].astype(jnp.float32)
        scale_ref[rows, :] = gain_ref[...] / (1.0 + jnp.exp(-gate))
        for h in range(LANES // HEAD_DIM):
            cols = slice(h * HEAD_DIM, (h + 1) * HEAD_DIM)
            q = queries[:, cols]
            scores = dot(q, keys_ref[rows, cols], ((1,), (1,)))
            scores = jnp.where(causal, scores, 0.0).astype(jnp.bfloat16)
            mixed = dot(scores, value_ref[rows, cols], ((1,), (0,)))
            if b == 1:
                mixed = mixed + wide_dot(q, first_ref[cols, :])
            inner_ref[rows, cols] = mixed


def final_body(queries_ref, inner_ref, scale_ref, state_ref, out_ref):
    for h in range(LANES // HEAD_DIM):
        cols = slice(h * HEAD_DIM, (h + 1) * HEAD_DIM)
        mixed = inner_ref[:, cols] + wide_dot(queries_ref[:, cols], state_ref[cols, :])
        power = jnp.mean(mixed * mixed, axis=-1, keepdims=True)
        out_ref[:, cols] = (mixed / jnp.sqrt(power + 1e-05) * scale_ref[:, cols]).astype(jnp.bfloat16)


def total_body(place_ref, part_ref, out_ref):
    total = part_ref[0]
    for m in range(1, part_ref.shape[0]):
        total = total + part_ref[m]
    for g in range(out_ref.shape[0]):
        out_ref[g] = jnp.where(place_ref[0] < g, total, 0.0)


def prefix_body(part_ref, before_ref, out_ref):
    state = before_ref[0]
    for g in range(1, before_ref.shape[0]):
        state = state + before_ref[g]
    for m in range(part_ref.shape[0]):
        out_ref[m] = state
        if m + 1 < part_ref.shape[0]:
            state = state + part_ref[m]


def cols_spec(rows):
    return pl.BlockSpec((rows, LANES), lambda i: (0, i))


STATE_SPEC = pl.BlockSpec((LANES, HEAD_DIM), lambda i: (i, 0))
PARAMS = pltpu.CompilerParams(vmem_limit_bytes=VMEM_LIMIT)


def per_device(query, key_in, value, gate, gain, ranges, inner_ranges):
    rows, width = query.shape
    steps = width // LANES
    tokens = cols_spec(rows)
    state_shape = jax.ShapeDtypeStruct((width, HEAD_DIM), jnp.float32)
    keys, first, total = pl.pallas_call(
        kv_body,
        grid=(steps,),
        in_specs=[tokens, tokens],
        out_specs=[tokens, STATE_SPEC, STATE_SPEC],
        out_shape=[jax.ShapeDtypeStruct((rows, width), jnp.bfloat16), state_shape, state_shape],
        compiler_params=PARAMS,
        name="block_kv",
    )(key_in, value)

    piece = width // inner_ranges
    parts = lax.all_to_all(total.reshape(inner_ranges, piece, HEAD_DIM), "seq", 0, 0, tiled=True)

    queries, inner, scale = pl.pallas_call(
        intra_body,
        grid=(steps,),
        in_specs=[tokens, tokens, tokens, tokens, pl.BlockSpec((1, LANES), lambda i: (0, i)), STATE_SPEC],
        out_specs=[tokens, tokens, tokens],
        out_shape=[
            jax.ShapeDtypeStruct((rows, width), jnp.bfloat16),
            jax.ShapeDtypeStruct((rows, width), jnp.float32),
            jax.ShapeDtypeStruct((rows, width), jnp.float32),
        ],
        compiler_params=PARAMS,
        name="within_block",
    )(query, keys, value, gate, gain.reshape(1, width), first)

    place = lax.axis_index("grp").astype(jnp.int32).reshape(1)
    range_total = pl.pallas_call(
        total_body,
        in_specs=[pl.BlockSpec(memory_space=pltpu.SMEM), pl.BlockSpec(memory_space=pltpu.VMEM)],
        out_shape=jax.ShapeDtypeStruct((ranges, piece, HEAD_DIM), jnp.float32),
        compiler_params=PARAMS,
        name="range_total",
    )(place, parts)
    before = lax.all_to_all(range_total, "grp", 0, 0, tiled=True)
    states = pl.pallas_call(
        prefix_body,
        out_shape=jax.ShapeDtypeStruct(parts.shape, jnp.float32),
        compiler_params=PARAMS,
        name="prefix",
    )(parts, before)
    state = lax.all_to_all(states, "seq", 0, 0, tiled=True).reshape(width, HEAD_DIM)

    return pl.pallas_call(
        final_body,
        grid=(steps,),
        in_specs=[tokens, tokens, tokens, STATE_SPEC],
        out_specs=tokens,
        out_shape=jax.ShapeDtypeStruct((rows, width), jnp.bfloat16),
        compiler_params=PARAMS,
        name="gated_norm",
    )(queries, inner, scale, state)


def solution(mesh):
    return jax.shard_map(
        functools.partial(per_device, ranges=mesh.shape["grp"], inner_ranges=mesh.shape["seq"]),
        mesh=mesh,
        in_specs=(
            P(("grp", "seq"), None),
            P(("grp", "seq"), None),
            P(("grp", "seq"), None),
            P(("grp", "seq"), None),
            P(),
        ),
        out_specs=P(("grp", "seq"), None),
        check_vma=False,
    )
```

time: 368 us -> 76.9 us (0.21)
  the two profiles are of different devices: /device:TPU:254 before, /device:TPU:32 now
where the time goes in v1:
time: 76.9 us; the launch traced here: 76.3 us
  waiting for transfers between devices  26.2 us (34%)
  starting transfers between devices  16.2 us (21%)
  Pallas kernels  12.2 us (16%)
  local copies, waits for them, and re-layouts  11.2 us (15%)
  blocking collectives  10.4 us (14%)
    all_to_all x1, waiting for transfers between devices, per_device(): lax.all_to_all(total.reshape(inner_ranges, piece, HEAD_DIM), 'seq', 0, 0,...  17.6 us
    all_to_all x1, starting transfers between devices, per_device(): lax.all_to_all(total.reshape(inner_ranges, piece, HEAD_DIM), 'seq', 0, 0,...  11.3 us
    unnamed x24, local copies, waits for them, and re-layouts  11.2 us
    all_to_all x1, blocking collectives, per_device(): before = lax.all_to_all(range_total, 'grp', 0, 0, tiled=True)  10.4 us
    all_to_all x1, waiting for transfers between devices, per_device(): lax.all_to_all(states, 'seq', 0, 0, tiled=True).reshape(width, HEAD_DIM)  8.61 us
    pallas_call x1, Pallas kernels, per_device(): pl.pallas_call(intra_body, grid=(steps,), in_specs=[tokens, tokens, token...  5.38 us
    all_to_all x1, starting transfers between devices, per_device(): lax.all_to_all(states, 'seq', 0, 0, tiled=True).reshape(width, HEAD_DIM)  4.86 us
    pallas_call x1, Pallas kernels, per_device(): pl.pallas_call(final_body, grid=(steps,), in_specs=[tokens, tokens, token...  3.25 us
  transfers between devices with their start and end apart: 2, of which 2 were waited for; matrix products, arithmetic and copies ran while one was open for 0% of the time, Pallas kernels for 7%

profile of v1, /device:TPU:32, one launch (start us, length us, event | category | flops | bytes accessed | tf_op | source)
XLA Modules:
  0.0 76.3 jit_solution(15047634919495073817)
XLA Ops:
  0.0 0.0 copy-start
  0.0 1.2 %copy-done = bf16[512,1024]{1,0:T(8,128)(2,1)S(1)} copy-done((bf16[512,1024]{1,0:T(8,128)(2,1)S(1)}, bf16[512,1024]{1,0:T(8,128)(2,1)}, u32[]{:S(2)}) %copy-start) | copy-done | bytes 1048600
  1.2 1.2 %copy-done.4 = bf16[512,1024]{1,0:T(8,128)(2,1)S(1)} copy-done((bf16[512,1024]{1,0:T(8,128)(2,1)S(1)}, bf16[512,1024]{1,0:T(8,128)(2,1)}, u32[]{:S(2)}) %copy-start.4) | copy-done | bytes 1048600
  2.5 2.7 %block_kv.1 = (bf16[512,1024]{1,0:T(8,128)(2,1)S(1)}, f32[1024,128]{1,0:T(8,128)S(1)}, f32[1024,128]{1,0:T(8,128)}) custom-call(bf16[512,1024]{1,0:T(8,128)(2,1)S(1)} %copy-done.4, bf16[512,1024]{1,0:T(8,128)(2,1)S(1)} %copy-done), custom_call_target="tpu_custom_call" | custom-call | tf_op jit(solution)/shard_map/block_kv/pallas_call | solution.py:109
  5.1 1.0 %copy-done.7 = bf16[512,1024]{1,0:T(8,128)(2,1)} copy-done((bf16[512,1024]{1,0:T(8,128)(2,1)}, bf16[512,1024]{1,0:T(8,128)(2,1)S(1)}, u32[]{:S(2)}) %copy-start.7) | copy-done | bytes 1048600
  6.1 11.3 %all-to-all-start = ((f32[32,32,128]{2,1,0:T(8,128)}), f32[32,32,128]{2,1,0:T(8,128)S(1)}, u32[]{:S(2)}, u32[]{:S(2)}) async-start(f32[32,32,128]{2,1,0:T(8,128)} %bitcast.1), calls=%async_computation | async-start | bytes 1048576 | tf_op jit(solution)/shard_map/all_to_all | solution.py:120
  17.4 17.6 %all-to-all-done.part_ref = f32[32,32,128]{2,1,0:T(8,128)S(1)} async-done(((f32[32,32,128]{2,1,0:T(8,128)}), f32[32,32,128]{2,1,0:T(8,128)S(1)}, u32[]{:S(2)}, u32[]{:S(2)}) %all-to-all-start) | async-done | bytes 524320 | tf_op jit(solution)/shard_map/all_to_all | solution.py:120
  35.1 0.1 range_total.1
  35.1 10.4 %all_to_all.15.before_ref = f32[8,32,128]{2,1,0:T(8,128)S(1)} all-to-all(f32[8,32,128]{2,1,0:T(8,128)S(1)} %range_total.1), channel_id=1, replica_groups=mesh['grp'=8,'seq'=32] {'grp'}, dimensions={0} | all-to-all | bytes 262144 | tf_op jit(solution)/shard_map/all_to_all | solution.py:144
  45.5 0.8 %prefix.1 = f32[32,32,128]{2,1,0:T(8,128)} custom-call(f32[32,32,128]{2,1,0:T(8,128)S(1)} %all-to-all-done.part_ref, f32[8,32,128]{2,1,0:T(8,128)S(1)} %all_to_all.15.before_ref), custom_call_target="tpu_custom_call" | custom-call | tf_op jit(solution)/shard_map/prefix/pallas_call | solution.py:145
  46.3 4.9 %all-to-all-start.2 = ((f32[32,32,128]{2,1,0:T(8,128)}), f32[32,32,128]{2,1,0:T(8,128)S(1)}, u32[]{:S(2)}, u32[]{:S(2)}) async-start(f32[32,32,128]{2,1,0:T(8,128)} %prefix.1), calls=%async_computation.2 | async-start | bytes 1048576 | tf_op jit(solution)/shard_map/all_to_all | solution.py:151
  51.2 0.0 copy-done.1
  51.2 0.0 copy-done.5
  51.2 0.0 copy-done.11
  51.2 0.0 copy-start.6
  51.3 1.2 %copy-done.6 = bf16[512,1024]{1,0:T(8,128)(2,1)S(1)} copy-done((bf16[512,1024]{1,0:T(8,128)(2,1)S(1)}, bf16[512,1024]{1,0:T(8,128)(2,1)}, u32[]{:S(2)}) %copy-start.6) | copy-done | bytes 1048600
  52.5 1.2 %copy-done.8 = bf16[512,1024]{1,0:T(8,128)(2,1)S(1)} copy-done((bf16[512,1024]{1,0:T(8,128)(2,1)S(1)}, bf16[512,1024]{1,0:T(8,128)(2,1)}, u32[]{:S(2)}) %copy-start.8) | copy-done | bytes 1048600
  53.7 5.4 %within_block.1 = (bf16[512,1024]{1,0:T(8,128)(2,1)S(1)}, f32[512,1024]{1,0:T(8,128)}, f32[512,1024]{1,0:T(8,128)}) custom-call(bf16[512,1024]{1,0:T(8,128)(2,1)S(1)} %copy-done.5, bf16[512,1024]{1,0:T(8,128)(2,1)S(1)} %copy-done.8, bf16[512,1024]{1,0:T(8,128)(2,1)S(1)} %copy-done.1, bf16[512,1024]{1,0:T(8,128)(2,1)S(1)} %copy-done.6, ...), custom_call_target="tpu_custom_call" | custom-call | tf_op jit(solution)/shard_map/within_block/pallas_call | solution.py:122
  59.1 1.0 %copy-done.9 = bf16[512,1024]{1,0:T(8,128)(2,1)} copy-done((bf16[512,1024]{1,0:T(8,128)(2,1)}, bf16[512,1024]{1,0:T(8,128)(2,1)S(1)}, u32[]{:S(2)}) %copy-start.9) | copy-done | bytes 1048600
  60.1 8.6 %all-to-all-done.2 = f32[32,32,128]{2,1,0:T(8,128)S(1)} async-done(((f32[32,32,128]{2,1,0:T(8,128)}), f32[32,32,128]{2,1,0:T(8,128)S(1)}, u32[]{:S(2)}, u32[]{:S(2)}) %all-to-all-start.2) | async-done | bytes 524320 | tf_op jit(solution)/shard_map/all_to_all | solution.py:151
  68.7 1.6 %copy-done.2 = f32[512,1024]{1,0:T(8,128)S(1)} copy-done((f32[512,1024]{1,0:T(8,128)S(1)}, f32[512,1024]{1,0:T(8,128)}, u32[]{:S(2)}) %copy-start.2) | copy-done | bytes 2097176
  70.3 1.6 %copy-done.3 = f32[512,1024]{1,0:T(8,128)S(1)} copy-done((f32[512,1024]{1,0:T(8,128)S(1)}, f32[512,1024]{1,0:T(8,128)}, u32[]{:S(2)}) %copy-start.3) | copy-done | bytes 2097176
  71.8 1.2 %copy-done.10 = bf16[512,1024]{1,0:T(8,128)(2,1)S(1)} copy-done((bf16[512,1024]{1,0:T(8,128)(2,1)S(1)}, bf16[512,1024]{1,0:T(8,128)(2,1)}, u32[]{:S(2)}) %copy-start.10) | copy-done | bytes 1048600
  73.1 3.2 %gated_norm.1 = bf16[512,1024]{1,0:T(8,128)(2,1)} custom-call(bf16[512,1024]{1,0:T(8,128)(2,1)S(1)} %copy-done.10, f32[512,1024]{1,0:T(8,128)S(1)} %copy-done.2, f32[512,1024]{1,0:T(8,128)S(1)} %copy-done.3, f32[1024,128]{1,0:T(8,128)S(1)} %bitcast.4), custom_call_target="tpu_custom_call" | custom-call | tf_op jit(solution)/shard_map/gated_norm/pallas_call | solution.py:153
  (10 shorter events, 0.0 us)
Async XLA Ops:
  0.0 1.2 %copy-start = (bf16[512,1024]{1,0:T(8,128)(2,1)S(1)}, bf16[512,1024]{1,0:T(8,128)(2,1)}, u32[]{:S(2)}) copy-start(bf16[512,1024]{1,0:T(8,128)(2,1)} %value_ref.3) | copy-start | bytes 3145732
  1.2 1.2 %copy-start.4 = (bf16[512,1024]{1,0:T(8,128)(2,1)S(1)}, bf16[512,1024]{1,0:T(8,128)(2,1)}, u32[]{:S(2)}) copy-start(bf16[512,1024]{1,0:T(8,128)(2,1)} %key_ref.1) | copy-start | bytes 3145732
  5.1 1.0 %copy-start.7 = (bf16[512,1024]{1,0:T(8,128)(2,1)}, bf16[512,1024]{1,0:T(8,128)(2,1)S(1)}, u32[]{:S(2)}) copy-start(bf16[512,1024]{1,0:T(8,128)(2,1)S(1)} %get-tuple-element.11.keys_ref) | copy-start | bytes 3145732
  6.1 45.1 %copy-start.1 = (bf16[512,1024]{1,0:T(8,128)(2,1)S(1)}, bf16[512,1024]{1,0:T(8,128)(2,1)}, u32[]{:S(2)}) copy-start(bf16[512,1024]{1,0:T(8,128)(2,1)} %value_ref.3) | copy-start | bytes 3145732
  6.1 45.1 %copy-start.5 = (bf16[512,1024]{1,0:T(8,128)(2,1)S(1)}, bf16[512,1024]{1,0:T(8,128)(2,1)}, u32[]{:S(2)}) copy-start(bf16[512,1024]{1,0:T(8,128)(2,1)} %query_ref.1) | copy-start | bytes 3145732
  6.1 45.1 %copy-start.11 = (f32[1024]{0:T(1024)S(1)}, f32[1024]{0:T(1024)}, u32[]{:S(2)}) copy-start(f32[1024]{0:T(1024)} %param.9) | copy-start | bytes 12292
  6.1 28.9 %all-to-all-start = ((f32[32,32,128]{2,1,0:T(8,128)}), f32[32,32,128]{2,1,0:T(8,128)S(1)}, u32[]{:S(2)}, u32[]{:S(2)}) async-start(f32[32,32,128]{2,1,0:T(8,128)} %bitcast.1), calls=%async_computation | async-start | bytes 1048576 | tf_op jit(solution)/shard_map/all_to_all | solution.py:120
  46.3 22.3 %all-to-all-start.2 = ((f32[32,32,128]{2,1,0:T(8,128)}), f32[32,32,128]{2,1,0:T(8,128)S(1)}, u32[]{:S(2)}, u32[]{:S(2)}) async-start(f32[32,32,128]{2,1,0:T(8,128)} %prefix.1), calls=%async_computation.2 | async-start | bytes 1048576 | tf_op jit(solution)/shard_map/all_to_all | solution.py:151
  51.2 1.2 %copy-start.6 = (bf16[512,1024]{1,0:T(8,128)(2,1)S(1)}, bf16[512,1024]{1,0:T(8,128)(2,1)}, u32[]{:S(2)}) copy-start(bf16[512,1024]{1,0:T(8,128)(2,1)} %gate_ref.1) | copy-start | bytes 3145732
  52.5 1.2 %copy-start.8 = (bf16[512,1024]{1,0:T(8,128)(2,1)S(1)}, bf16[512,1024]{1,0:T(8,128)(2,1)}, u32[]{:S(2)}) copy-start(bf16[512,1024]{1,0:T(8,128)(2,1)} %copy-done.7) | copy-start | bytes 3145732
  59.1 1.0 %copy-start.9 = (bf16[512,1024]{1,0:T(8,128)(2,1)}, bf16[512,1024]{1,0:T(8,128)(2,1)S(1)}, u32[]{:S(2)}) copy-start(bf16[512,1024]{1,0:T(8,128)(2,1)S(1)} %get-tuple-element.13.queries_ref) | copy-start | bytes 3145732
  68.7 1.6 %copy-start.2 = (f32[512,1024]{1,0:T(8,128)S(1)}, f32[512,1024]{1,0:T(8,128)}, u32[]{:S(2)}) copy-start(f32[512,1024]{1,0:T(8,128)} %get-tuple-element.14.inner_ref) | copy-start | bytes 6291460
  70.3 1.6 %copy-start.3 = (f32[512,1024]{1,0:T(8,128)S(1)}, f32[512,1024]{1,0:T(8,128)}, u32[]{:S(2)}) copy-start(f32[512,1024]{1,0:T(8,128)} %get-tuple-element.15.scale_ref) | copy-start | bytes 6291460
  71.8 1.2 %copy-start.10 = (bf16[512,1024]{1,0:T(8,128)(2,1)S(1)}, bf16[512,1024]{1,0:T(8,128)(2,1)}, u32[]{:S(2)}) copy-start(bf16[512,1024]{1,0:T(8,128)(2,1)} %copy-done.9) | copy-start | bytes 3145732

commit v2 on v1

v2 whole, which is shorter than its diff:
```python
import functools

import jax
import jax.numpy as jnp
from jax import lax
from jax.experimental import pallas as pl
from jax.experimental.pallas import tpu as pltpu
from jax.sharding import PartitionSpec as P

HEADS = 8
HEAD_DIM = 128
BLOCK = 256
LANES = 2 * HEAD_DIM


def silu(u):
    u = u.astype(jnp.float32)
    return (u / (1.0 + jnp.exp(-u))).astype(jnp.bfloat16)


def dot(a, b, contract):
    return lax.dot_general(a, b, ((contract[0], contract[1]), ((), ())), preferred_element_type=jnp.float32)


def wide_dot(a, state):
    high = state.astype(jnp.bfloat16)
    low = (state - high.astype(jnp.float32)).astype(jnp.bfloat16)
    return dot(jnp.concatenate([a, a], axis=1), jnp.concatenate([high, low], axis=0), ((1,), (0,)))


def stream(sources, targets, sems):
    pieces = []
    for i in range(sources[0].shape[1] // LANES):
        cols = pl.ds(i * LANES, LANES)
        piece = [
            pltpu.make_async_copy(source.at[:, cols], target.at[:, cols], sem.at[i])
            for source, target, sem in zip(sources, targets, sems)
        ]
        for copy in piece:
            copy.start()
        pieces.append(piece)
    return pieces


def heads_of(i):
    for h in range(i * LANES // HEAD_DIM, (i + 1) * LANES // HEAD_DIM):
        yield slice(h * HEAD_DIM, (h + 1) * HEAD_DIM)


def blocks_of(rows):
    return [slice(b * BLOCK, (b + 1) * BLOCK) for b in range(rows // BLOCK)]


def kv_body(key_hbm, value_hbm, total_ref, key_ref, value_ref, key_sem, value_sem):
    pieces = stream((key_hbm, value_hbm), (key_ref, value_ref), (key_sem, value_sem))
    for i, piece in enumerate(pieces):
        for copy in piece:
            copy.wait()
        for cols in heads_of(i):
            total_ref[cols, :] = dot(silu(key_ref[:, cols]), value_ref[:, cols], ((0,), (0,)))


def intra_body(
    query_hbm, key_hbm, value_hbm, gate_hbm, gain_ref, queries_ref, inner_ref, scale_ref,
    query_ref, key_ref, value_ref, gate_ref, query_sem, key_sem, value_sem, gate_sem,
):
    pieces = stream(
        (query_hbm, key_hbm, value_hbm, gate_hbm),
        (query_ref, key_ref, value_ref, gate_ref),
        (query_sem, key_sem, value_sem, gate_sem),
    )
    row = lax.broadcasted_iota(jnp.int32, (BLOCK, BLOCK), 0)
    col = lax.broadcasted_iota(jnp.int32, (BLOCK, BLOCK), 1)
    causal = row >= col
    for i, piece in enumerate(pieces):
        for copy in piece:
            copy.wait()
        for cols in heads_of(i):
            state = None
            for rows in blocks_of(query_hbm.shape[0]):
                q = silu(query_ref[rows, cols])
                k = silu(key_ref[rows, cols])
                v = value_ref[rows, cols]
                queries_ref[rows, cols] = q
                gate = gate_ref[rows, cols].astype(jnp.float32)
                scale_ref[rows, cols] = gain_ref[:, cols] / (1.0 + jnp.exp(-gate))
                scores = jnp.where(causal, dot(q, k, ((1,), (1,))), 0.0).astype(jnp.bfloat16)
                mixed = dot(scores, v, ((1,), (0,)))
                if state is not None:
                    mixed = mixed + wide_dot(q, state)
                inner_ref[rows, cols] = mixed
                if rows.stop < query_hbm.shape[0]:
                    block_kv = dot(k, v, ((0,), (0,)))
                    state = block_kv if state is None else state + block_kv


def final_body(queries_ref, inner_ref, scale_ref, state_ref, out_hbm, out_ref, sem):
    stores = []
    for i in range(queries_ref.shape[1] // LANES):
        for cols in heads_of(i):
            mixed = inner_ref[:, cols] + wide_dot(queries_ref[:, cols], state_ref[cols, :])
            power = jnp.mean(mixed * mixed, axis=-1, keepdims=True)
            out_ref[:, cols] = (mixed * (1.0 / jnp.sqrt(power + 1e-05)) * scale_ref[:, cols]).astype(jnp.bfloat16)
        cols = pl.ds(i * LANES, LANES)
        store = pltpu.make_async_copy(out_ref.at[:, cols], out_hbm.at[:, cols], sem.at[i])
        store.start()
        stores.append(store)
    for store in stores:
        store.wait()


def total_body(place_ref, part_ref, out_ref):
    total = part_ref[0]
    for m in range(1, part_ref.shape[0]):
        total = total + part_ref[m]
    for g in range(out_ref.shape[0]):
        out_ref[g] = jnp.where(place_ref[0] < g, total, 0.0)


def prefix_body(part_ref, before_ref, out_ref):
    state = before_ref[0]
    for g in range(1, before_ref.shape[0]):
        state = state + before_ref[g]
    for m in range(part_ref.shape[0]):
        out_ref[m] = state
        if m + 1 < part_ref.shape[0]:
            state = state + part_ref[m]


HBM = pl.BlockSpec(memory_space=pltpu.HBM)
VMEM = pl.BlockSpec(memory_space=pltpu.VMEM)


def params(mib):
    return pltpu.CompilerParams(vmem_limit_bytes=mib * 1024 * 1024)


def per_device(query, key_in, value, gate, gain, ranges, inner_ranges):
    rows, width = query.shape
    steps = width // LANES
    tokens = pltpu.VMEM((rows, width), jnp.bfloat16)
    wide_tokens = pltpu.VMEM((rows, width), jnp.float32)
    sems = pltpu.SemaphoreType.DMA((steps,))
    query, key_in, value, gate = (pltpu.with_memory_space_constraint(a, pltpu.HBM) for a in (query, key_in, value, gate))
    total = pl.pallas_call(
        kv_body,
        in_specs=[HBM, HBM],
        out_specs=VMEM,
        out_shape=jax.ShapeDtypeStruct((width, HEAD_DIM), jnp.float32),
        scratch_shapes=[tokens, tokens, sems, sems],
        compiler_params=params(16),
        name="range_part",
    )(key_in, value)

    piece = width // inner_ranges
    parts = lax.all_to_all(total.reshape(inner_ranges, piece, HEAD_DIM), "seq", 0, 0, tiled=True)

    queries, inner, scale = pl.pallas_call(
        intra_body,
        in_specs=[HBM, HBM, HBM, HBM, VMEM],
        out_specs=[VMEM] * 3,
        out_shape=[
            jax.ShapeDtypeStruct((rows, width), jnp.bfloat16),
            jax.ShapeDtypeStruct((rows, width), jnp.float32),
            jax.ShapeDtypeStruct((rows, width), jnp.float32),
        ],
        scratch_shapes=[tokens] * 4 + [sems] * 4,
        compiler_params=params(16),
        name="within_block",
    )(query, key_in, value, gate, gain.reshape(1, width))
    parts, queries, inner, scale = lax.optimization_barrier((parts, queries, inner, scale))

    place = lax.axis_index("grp").astype(jnp.int32).reshape(1)
    range_total = pl.pallas_call(
        total_body,
        in_specs=[pl.BlockSpec(memory_space=pltpu.SMEM), VMEM],
        out_specs=VMEM,
        out_shape=jax.ShapeDtypeStruct((ranges, piece, HEAD_DIM), jnp.float32),
        compiler_params=params(16),
        name="range_total",
    )(place, parts)
    before = lax.all_to_all(range_total, "grp", 0, 0, tiled=True)
    states = pl.pallas_call(
        prefix_body,
        in_specs=[VMEM, VMEM],
        out_specs=VMEM,
        out_shape=jax.ShapeDtypeStruct(parts.shape, jnp.float32),
        compiler_params=params(16),
        name="prefix",
    )(parts, before)
    state = lax.all_to_all(states, "seq", 0, 0, tiled=True).reshape(width, HEAD_DIM)

    return pl.pallas_call(
        final_body,
        in_specs=[VMEM] * 4,
        out_specs=HBM,
        out_shape=jax.ShapeDtypeStruct((rows, width), jnp.bfloat16),
        scratch_shapes=[tokens, pltpu.SemaphoreType.DMA((steps,))],
        compiler_params=params(16),
        name="gated_norm",
    )(queries, inner, scale, state)


def solution(mesh):
    return jax.shard_map(
        functools.partial(per_device, ranges=mesh.shape["grp"], inner_ranges=mesh.shape["seq"]),
        mesh=mesh,
        in_specs=(
            P(("grp", "seq"), None),
            P(("grp", "seq"), None),
            P(("grp", "seq"), None),
            P(("grp", "seq"), None),
            P(),
        ),
        out_specs=P(("grp", "seq"), None),
        check_vma=False,
    )
```

time: 76.9 us -> 67.4 us (0.88)
  blocking collectives: 10.4 us -> 32.8 us
  waiting for transfers between devices: 26.2 us -> 10 us
  local copies, waits for them, and re-layouts: 11.2 us -> 2.32 us
  starting transfers between devices: 16.2 us -> 11.2 us
  Pallas kernels: 12.2 us -> 10.8 us
    all_to_all x0 -> x1, blocking collectives: none -> 22.1 us  [per_device(): lax.all_to_all(states, 'seq', 0, 0, tiled=True).reshape(width, HEAD_DIM)]
    unnamed x24 -> x10, local copies, waits for them, and re-layouts: 11.2 us -> 2.32 us
    all_to_all x1 -> x0, waiting for transfers between devices: 8.61 us -> none  [per_device(): lax.all_to_all(states, 'seq', 0, 0, tiled=True).reshape(width, HEAD_DIM)]
    all_to_all x1, waiting for transfers between devices: 17.6 us -> 10 us  [per_device(): lax.all_to_all(total.reshape(inner_ranges, piece, HEAD_DIM), 'seq', 0, 0,...]
    all_to_all x1 -> x0, starting transfers between devices: 4.86 us -> none  [per_device(): lax.all_to_all(states, 'seq', 0, 0, tiled=True).reshape(width, HEAD_DIM)]
    pallas_call x4, Pallas kernels: 12.1 us -> 10.7 us  [the longest x1 5.24 us: per_device(): pl.pallas_call(intra_body, in_specs=[HBM, HBM, HBM, HBM, VMEM], out_specs...]
  transfers between devices with their start and end apart: 2 -> 1, of which waited for: 2 -> 1; matrix products, arithmetic and copies ran while one was open for 0% -> 0% of each run, Pallas kernels for 7% -> 8%
where the time goes in v2:
time: 67.4 us; the launch traced here: 67.1 us
  blocking collectives  32.8 us (49%)
  starting transfers between devices  11.2 us (17%)
  Pallas kernels  10.8 us (16%)
  waiting for transfers between devices  10 us (15%)
  local copies, waits for them, and re-layouts  2.32 us (3%)
    all_to_all x1, blocking collectives, per_device(): lax.all_to_all(states, 'seq', 0, 0, tiled=True).reshape(width, HEAD_DIM)  22.1 us
    all_to_all x1, starting transfers between devices, per_device(): lax.all_to_all(total.reshape(inner_ranges, piece, HEAD_DIM), 'seq', 0, 0,...  11.2 us
    all_to_all x1, blocking collectives, per_device(): before = lax.all_to_all(range_total, 'grp', 0, 0, tiled=True)  10.7 us
    all_to_all x1, waiting for transfers between devices, per_device(): lax.all_to_all(total.reshape(inner_ranges, piece, HEAD_DIM), 'seq', 0, 0,...  10 us
    pallas_call x1, Pallas kernels, per_device(): pl.pallas_call(intra_body, in_specs=[HBM, HBM, HBM, HBM, VMEM], out_specs...  5.24 us
    pallas_call x1, Pallas kernels, per_device(): pl.pallas_call(kv_body, in_specs=[HBM, HBM], out_specs=VMEM, out_shape=ja...  3.38 us
    unnamed x10, local copies, waits for them, and re-layouts  2.32 us
    pallas_call x1, Pallas kernels, per_device(): pl.pallas_call(final_body, in_specs=[VMEM] * 4, out_specs=HBM, out_shape=...  2.04 us
  transfers between devices with their start and end apart: 1, of which 1 were waited for; matrix products, arithmetic and copies ran while one was open for 0% of the time, Pallas kernels for 8%

profile of v2, /device:TPU:32, one launch (start us, length us, event | category | flops | bytes accessed | tf_op | source)
XLA Modules:
  0.0 67.1 jit_solution(17666626223739246336)
XLA Ops:
  0.0 0.0 copy-start.4
  0.0 3.4 %range_part.1 = f32[1024,128]{1,0:T(8,128)} custom-call(bf16[512,1024]{1,0:T(8,128)(2,1)} %key_hbm.3, bf16[512,1024]{1,0:T(8,128)(2,1)} %value_hbm.3), custom_call_target="tpu_custom_call" | custom-call | tf_op jit(solution)/shard_map/range_part/pallas_call | solution.py:145
  3.4 11.2 %all-to-all-start = ((f32[32,32,128]{2,1,0:T(8,128)}), f32[32,32,128]{2,1,0:T(8,128)S(1)}, u32[]{:S(2)}, u32[]{:S(2)}) async-start(f32[32,32,128]{2,1,0:T(8,128)} %bitcast), calls=%async_computation | async-start | bytes 1048576 | tf_op jit(solution)/shard_map/all_to_all | solution.py:156
  14.6 0.0 copy-done.4
  14.6 5.2 %within_block.1 = (bf16[512,1024]{1,0:T(8,128)(2,1)S(1)}, f32[512,1024]{1,0:T(8,128)S(1)}, f32[512,1024]{1,0:T(8,128)S(1)}) custom-call(bf16[512,1024]{1,0:T(8,128)(2,1)} %query_hbm.1, bf16[512,1024]{1,0:T(8,128)(2,1)} %key_hbm.3, bf16[512,1024]{1,0:T(8,128)(2,1)} %value_hbm.3, bf16[512,1024]{1,0:T(8,128)(2,1)} %gate_hbm.1, f32[1,1024]{1,0:T(1,128)S(1)} %bitcast.5), custom_call_target="tpu_custom_call" | custom-call | tf_op jit(solution)/shard_map/within_block/pallas_call | solution.py:158
  19.9 0.0 copy-start
  19.9 1.3 %copy-done = f32[512,1024]{1,0:T(8,128)} copy-done((f32[512,1024]{1,0:T(8,128)}, f32[512,1024]{1,0:T(8,128)S(1)}, u32[]{:S(2)}) %copy-start) | copy-done | bytes 2097176
  21.2 0.0 copy-start.2
  21.2 1.0 %copy-done.2 = bf16[512,1024]{1,0:T(8,128)(2,1)} copy-done((bf16[512,1024]{1,0:T(8,128)(2,1)}, bf16[512,1024]{1,0:T(8,128)(2,1)S(1)}, u32[]{:S(2)}) %copy-start.2) | copy-done | bytes 1048600
  22.2 10.0 %all-to-all-done.part_ref = f32[32,32,128]{2,1,0:T(8,128)S(1)} async-done(((f32[32,32,128]{2,1,0:T(8,128)}), f32[32,32,128]{2,1,0:T(8,128)S(1)}, u32[]{:S(2)}, u32[]{:S(2)}) %all-to-all-start) | async-done | bytes 524320 | tf_op jit(solution)/shard_map/all_to_all | solution.py:156
  32.2 0.0 copy-start.1
  32.2 0.0 copy-start.3
  32.2 0.1 range_total.1
  32.3 10.7 %all_to_all.15.before_ref = f32[8,32,128]{2,1,0:T(8,128)S(1)} all-to-all(f32[8,32,128]{2,1,0:T(8,128)S(1)} %range_total.1), channel_id=1, replica_groups=mesh['grp'=8,'seq'=32] {'grp'}, dimensions={0} | all-to-all | bytes 262144 | tf_op jit(solution)/shard_map/all_to_all | solution.py:182
  43.0 22.1 %all_to_all.16 = f32[32,32,128]{2,1,0:T(8,128)S(1)} all-to-all(f32[32,32,128]{2,1,0:T(8,128)S(1)} %prefix.1), channel_id=1, replica_groups=mesh['grp'=8,'seq'=32] {'seq'}, dimensions={0} | all-to-all | bytes 1048576 | tf_op jit(solution)/shard_map/all_to_all | solution.py:191
  65.1 0.0 copy-done.1
  65.1 0.0 copy-done.3
  65.1 2.0 %gated_norm.1 = bf16[512,1024]{1,0:T(8,128)(2,1)} custom-call(bf16[512,1024]{1,0:T(8,128)(2,1)S(1)} %copy-done.3, f32[512,1024]{1,0:T(8,128)S(1)} %get-tuple-element.16.inner_ref, f32[512,1024]{1,0:T(8,128)S(1)} %copy-done.1, f32[1024,128]{1,0:T(8,128)S(1)} %bitcast.4), custom_call_target="tpu_custom_call" | custom-call | tf_op jit(solution)/shard_map/gated_norm/pallas_call | solution.py:193
  (1 shorter events, 0.0 us)
Async XLA Ops:
  0.0 14.6 %copy-start.4 = (f32[1024]{0:T(1024)S(1)}, f32[1024]{0:T(1024)}, u32[]{:S(2)}) copy-start(f32[1024]{0:T(1024)} %param.9) | copy-start | bytes 12292
  3.4 28.8 %all-to-all-start = ((f32[32,32,128]{2,1,0:T(8,128)}), f32[32,32,128]{2,1,0:T(8,128)S(1)}, u32[]{:S(2)}, u32[]{:S(2)}) async-start(f32[32,32,128]{2,1,0:T(8,128)} %bitcast), calls=%async_computation | async-start | bytes 1048576 | tf_op jit(solution)/shard_map/all_to_all | solution.py:156
  19.9 1.3 %copy-start = (f32[512,1024]{1,0:T(8,128)}, f32[512,1024]{1,0:T(8,128)S(1)}, u32[]{:S(2)}) copy-start(f32[512,1024]{1,0:T(8,128)S(1)} %get-tuple-element.17.scale_ref) | copy-start | bytes 6291460
  21.2 1.0 %copy-start.2 = (bf16[512,1024]{1,0:T(8,128)(2,1)}, bf16[512,1024]{1,0:T(8,128)(2,1)S(1)}, u32[]{:S(2)}) copy-start(bf16[512,1024]{1,0:T(8,128)(2,1)S(1)} %get-tuple-element.15.queries_ref) | copy-start | bytes 3145732
  32.2 32.9 %copy-start.1 = (f32[512,1024]{1,0:T(8,128)S(1)}, f32[512,1024]{1,0:T(8,128)}, u32[]{:S(2)}) copy-start(f32[512,1024]{1,0:T(8,128)} %copy-done) | copy-start | bytes 6291460
  32.2 32.9 %copy-start.3 = (bf16[512,1024]{1,0:T(8,128)(2,1)S(1)}, bf16[512,1024]{1,0:T(8,128)(2,1)}, u32[]{:S(2)}) copy-start(bf16[512,1024]{1,0:T(8,128)(2,1)} %copy-done.2) | copy-start | bytes 3145732

commit v3 on v2

--- a/solution.py
+++ b/solution.py
@@ -11,6 +11,7 @@
 HEAD_DIM = 128
 BLOCK = 256
 LANES = 2 * HEAD_DIM
+KV_LANES = 4 * HEAD_DIM
 
 
 def silu(u):
@@ -28,10 +29,10 @@
     return dot(jnp.concatenate([a, a], axis=1), jnp.concatenate([high, low], axis=0), ((1,), (0,)))
 
 
-def stream(sources, targets, sems):
+def stream(sources, targets, sems, lanes):
     pieces = []
-    for i in range(sources[0].shape[1] // LANES):
-        cols = pl.ds(i * LANES, LANES)
+    for i in range(sources[0].shape[1] // lanes):
+        cols = pl.ds(i * lanes, lanes)
         piece = [
             pltpu.make_async_copy(source.at[:, cols], target.at[:, cols], sem.at[i])
             for source, target, sem in zip(sources, targets, sems)
@@ -42,8 +43,8 @@
     return pieces
 
 
-def heads_of(i):
-    for h in range(i * LANES // HEAD_DIM, (i + 1) * LANES // HEAD_DIM):
+def heads_of(i, lanes):
+    for h in range(i * lanes // HEAD_DIM, (i + 1) * lanes // HEAD_DIM):
         yield slice(h * HEAD_DIM, (h + 1) * HEAD_DIM)
 
 
@@ -51,13 +52,20 @@
     return [slice(b * BLOCK, (b + 1) * BLOCK) for b in range(rows // BLOCK)]
 
 
-def kv_body(key_hbm, value_hbm, total_ref, key_ref, value_ref, key_sem, value_sem):
-    pieces = stream((key_hbm, value_hbm), (key_ref, value_ref), (key_sem, value_sem))
+def kv_body(key_hbm, value_hbm, total_hbm, key_ref, value_ref, total_ref, key_sem, value_sem, total_sem):
+    pieces = stream((key_hbm, value_hbm), (key_ref, value_ref), (key_sem, value_sem), KV_LANES)
+    stores = []
     for i, piece in enumerate(pieces):
         for copy in piece:
             copy.wait()
-        for cols in heads_of(i):
+        for cols in heads_of(i, KV_LANES):
             total_ref[cols, :] = dot(silu(key_ref[:, cols]), value_ref[:, cols], ((0,), (0,)))
+        done = pl.ds(i * KV_LANES, KV_LANES)
+        store = pltpu.make_async_copy(total_ref.at[done, :], total_hbm.at[done, :], total_sem.at[i])
+        store.start()
+        stores.append(store)
+    for store in stores:
+        store.wait()
 
 
 def intra_body(
@@ -68,6 +76,7 @@
         (query_hbm, key_hbm, value_hbm, gate_hbm),
         (query_ref, key_ref, value_ref, gate_ref),
         (query_sem, key_sem, value_sem, gate_sem),
+        LANES,
     )
     row = lax.broadcasted_iota(jnp.int32, (BLOCK, BLOCK), 0)
     col = lax.broadcasted_iota(jnp.int32, (BLOCK, BLOCK), 1)
@@ -75,7 +84,7 @@
     for i, piece in enumerate(pieces):
         for copy in piece:
             copy.wait()
-        for cols in heads_of(i):
+        for cols in heads_of(i, LANES):
             state = None
             for rows in blocks_of(query_hbm.shape[0]):
                 q = silu(query_ref[rows, cols])
@@ -97,10 +106,10 @@
 def final_body(queries_ref, inner_ref, scale_ref, state_ref, out_hbm, out_ref, sem):
     stores = []
     for i in range(queries_ref.shape[1] // LANES):
-        for cols in heads_of(i):
+        for cols in heads_of(i, LANES):
             mixed = inner_ref[:, cols] + wide_dot(queries_ref[:, cols], state_ref[cols, :])
             power = jnp.mean(mixed * mixed, axis=-1, keepdims=True)
-            out_ref[:, cols] = (mixed * (1.0 / jnp.sqrt(power + 1e-05)) * scale_ref[:, cols]).astype(jnp.bfloat16)
+            out_ref[:, cols] = (mixed * lax.rsqrt(power + 1e-05) * scale_ref[:, cols]).astype(jnp.bfloat16)
         cols = pl.ds(i * LANES, LANES)
         store = pltpu.make_async_copy(out_ref.at[:, cols], out_hbm.at[:, cols], sem.at[i])
         store.start()
@@ -145,9 +154,10 @@
     total = pl.pallas_call(
         kv_body,
         in_specs=[HBM, HBM],
-        out_specs=VMEM,
-        out_shape=jax.ShapeDtypeStruct((width, HEAD_DIM), jnp.float32),
-        scratch_shapes=[tokens, tokens, sems, sems],
+        out_specs=HBM,
+        out_shape=pltpu.HBM((width, HEAD_DIM), jnp.float32),
+        scratch_shapes=[tokens, tokens, pltpu.VMEM((width, HEAD_DIM), jnp.float32)]
+        + [pltpu.SemaphoreType.DMA((width // KV_LANES,))] * 3,
         compiler_params=params(16),
         name="range_part",
     )(key_in, value)

time: 67.4 us -> 66.7 us (0.990)
  Pallas kernels: 10.8 us -> 10.1 us
where the time goes in v3:
time: 66.7 us; the launch traced here: 66.4 us
  blocking collectives  32.8 us (49%)
  starting transfers between devices  11.2 us (17%)
  Pallas kernels  10.1 us (15%)
  waiting for transfers between devices  10 us (15%)
  local copies, waits for them, and re-layouts  2.32 us (3%)
    all_to_all x1, blocking collectives, per_device(): lax.all_to_all(states, 'seq', 0, 0, tiled=True).reshape(width, HEAD_DIM)  22.1 us
    all_to_all x1, starting transfers between devices, per_device(): lax.all_to_all(total.reshape(inner_ranges, piece, HEAD_DIM), 'seq', 0, 0,...  11.2 us
    all_to_all x1, blocking collectives, per_device(): before = lax.all_to_all(range_total, 'grp', 0, 0, tiled=True)  10.7 us
    all_to_all x1, waiting for transfers between devices, per_device(): lax.all_to_all(total.reshape(inner_ranges, piece, HEAD_DIM), 'seq', 0, 0,...  10 us
    pallas_call x1, Pallas kernels, per_device(): pl.pallas_call(intra_body, in_specs=[HBM, HBM, HBM, HBM, VMEM], out_specs...  5.25 us
    pallas_call x1, Pallas kernels, per_device(): pl.pallas_call(kv_body, in_specs=[HBM, HBM], out_specs=HBM, out_shape=plt...  3.06 us
    unnamed x10, local copies, waits for them, and re-layouts  2.32 us
    pallas_call x1, Pallas kernels, per_device(): pl.pallas_call(final_body, in_specs=[VMEM] * 4, out_specs=HBM, out_shape=...  1.65 us
  transfers between devices with their start and end apart: 1, of which 1 were waited for; matrix products, arithmetic and copies ran while one was open for 0% of the time, Pallas kernels for 8%

profile of v3, /device:TPU:32, one launch (start us, length us, event | category | flops | bytes accessed | tf_op | source)
XLA Modules:
  0.0 66.4 jit_solution(6701128695451693852)
XLA Ops:
  0.0 0.0 copy-start.4
  0.0 3.1 %range_part.1 = f32[1024,128]{1,0:T(8,128)} custom-call(bf16[512,1024]{1,0:T(8,128)(2,1)} %key_hbm.3, bf16[512,1024]{1,0:T(8,128)(2,1)} %value_hbm.3), custom_call_target="tpu_custom_call" | custom-call | tf_op jit(solution)/shard_map/range_part/pallas_call | solution.py:154
  3.1 11.2 %all-to-all-start = ((f32[32,32,128]{2,1,0:T(8,128)}), f32[32,32,128]{2,1,0:T(8,128)S(1)}, u32[]{:S(2)}, u32[]{:S(2)}) async-start(f32[32,32,128]{2,1,0:T(8,128)} %bitcast.6), calls=%async_computation | async-start | bytes 1048576 | tf_op jit(solution)/shard_map/all_to_all | solution.py:166
  14.3 0.0 copy-done.4
  14.3 5.2 %within_block.1 = (bf16[512,1024]{1,0:T(8,128)(2,1)S(1)}, f32[512,1024]{1,0:T(8,128)S(1)}, f32[512,1024]{1,0:T(8,128)S(1)}) custom-call(bf16[512,1024]{1,0:T(8,128)(2,1)} %query_hbm.1, bf16[512,1024]{1,0:T(8,128)(2,1)} %key_hbm.3, bf16[512,1024]{1,0:T(8,128)(2,1)} %value_hbm.3, bf16[512,1024]{1,0:T(8,128)(2,1)} %gate_hbm.1, f32[1,1024]{1,0:T(1,128)S(1)} %bitcast.5), custom_call_target="tpu_custom_call" | custom-call | tf_op jit(solution)/shard_map/within_block/pallas_call | solution.py:168
  19.6 0.0 copy-start
  19.6 1.3 %copy-done = f32[512,1024]{1,0:T(8,128)} copy-done((f32[512,1024]{1,0:T(8,128)}, f32[512,1024]{1,0:T(8,128)S(1)}, u32[]{:S(2)}) %copy-start) | copy-done | bytes 2097176
  20.9 0.0 copy-start.2
  20.9 1.0 %copy-done.2 = bf16[512,1024]{1,0:T(8,128)(2,1)} copy-done((bf16[512,1024]{1,0:T(8,128)(2,1)}, bf16[512,1024]{1,0:T(8,128)(2,1)S(1)}, u32[]{:S(2)}) %copy-start.2) | copy-done | bytes 1048600
  21.9 10.0 %all-to-all-done.part_ref = f32[32,32,128]{2,1,0:T(8,128)S(1)} async-done(((f32[32,32,128]{2,1,0:T(8,128)}), f32[32,32,128]{2,1,0:T(8,128)S(1)}, u32[]{:S(2)}, u32[]{:S(2)}) %all-to-all-start) | async-done | bytes 524320 | tf_op jit(solution)/shard_map/all_to_all | solution.py:166
  31.9 0.0 copy-start.1
  31.9 0.0 copy-start.3
  31.9 0.1 range_total.1
  32.0 10.7 %all_to_all.15.before_ref = f32[8,32,128]{2,1,0:T(8,128)S(1)} all-to-all(f32[8,32,128]{2,1,0:T(8,128)S(1)} %range_total.1), channel_id=1, replica_groups=mesh['grp'=8,'seq'=32] {'grp'}, dimensions={0} | all-to-all | bytes 262144 | tf_op jit(solution)/shard_map/all_to_all | solution.py:192
  42.7 22.1 %all_to_all.16 = f32[32,32,128]{2,1,0:T(8,128)S(1)} all-to-all(f32[32,32,128]{2,1,0:T(8,128)S(1)} %prefix.1), channel_id=1, replica_groups=mesh['grp'=8,'seq'=32] {'seq'}, dimensions={0} | all-to-all | bytes 1048576 | tf_op jit(solution)/shard_map/all_to_all | solution.py:201
  64.8 0.0 copy-done.1
  64.8 0.0 copy-done.3
  64.8 1.6 %gated_norm.1 = bf16[512,1024]{1,0:T(8,128)(2,1)} custom-call(bf16[512,1024]{1,0:T(8,128)(2,1)S(1)} %copy-done.3, f32[512,1024]{1,0:T(8,128)S(1)} %get-tuple-element.16.inner_ref, f32[512,1024]{1,0:T(8,128)S(1)} %copy-done.1, f32[1024,128]{1,0:T(8,128)S(1)} %bitcast.4), custom_call_target="tpu_custom_call" | custom-call | tf_op jit(solution)/shard_map/gated_norm/pallas_call | solution.py:203
  (1 shorter events, 0.0 us)
Async XLA Ops:
  0.0 14.3 %copy-start.4 = (f32[1024]{0:T(1024)S(1)}, f32[1024]{0:T(1024)}, u32[]{:S(2)}) copy-start(f32[1024]{0:T(1024)} %param.9) | copy-start | bytes 12292
  3.1 28.8 %all-to-all-start = ((f32[32,32,128]{2,1,0:T(8,128)}), f32[32,32,128]{2,1,0:T(8,128)S(1)}, u32[]{:S(2)}, u32[]{:S(2)}) async-start(f32[32,32,128]{2,1,0:T(8,128)} %bitcast.6), calls=%async_computation | async-start | bytes 1048576 | tf_op jit(solution)/shard_map/all_to_all | solution.py:166
  19.6 1.3 %copy-start = (f32[512,1024]{1,0:T(8,128)}, f32[512,1024]{1,0:T(8,128)S(1)}, u32[]{:S(2)}) copy-start(f32[512,1024]{1,0:T(8,128)S(1)} %get-tuple-element.17.scale_ref) | copy-start | bytes 6291460
  20.9 1.0 %copy-start.2 = (bf16[512,1024]{1,0:T(8,128)(2,1)}, bf16[512,1024]{1,0:T(8,128)(2,1)S(1)}, u32[]{:S(2)}) copy-start(bf16[512,1024]{1,0:T(8,128)(2,1)S(1)} %get-tuple-element.15.queries_ref) | copy-start | bytes 3145732
  31.9 32.9 %copy-start.1 = (f32[512,1024]{1,0:T(8,128)S(1)}, f32[512,1024]{1,0:T(8,128)}, u32[]{:S(2)}) copy-start(f32[512,1024]{1,0:T(8,128)} %copy-done) | copy-start | bytes 6291460
  31.9 32.9 %copy-start.3 = (bf16[512,1024]{1,0:T(8,128)(2,1)S(1)}, bf16[512,1024]{1,0:T(8,128)(2,1)}, u32[]{:S(2)}) copy-start(bf16[512,1024]{1,0:T(8,128)(2,1)} %copy-done.2) | copy-start | bytes 3145732

commit v4 on v3

--- a/solution.py
+++ b/solution.py
@@ -118,18 +118,20 @@
         store.wait()
 
 
-def total_body(place_ref, part_ref, out_ref):
+def total_body(part_ref, out_ref):
     total = part_ref[0]
     for m in range(1, part_ref.shape[0]):
         total = total + part_ref[m]
-    for g in range(out_ref.shape[0]):
-        out_ref[g] = jnp.where(place_ref[0] < g, total, 0.0)
-
-
-def prefix_body(part_ref, before_ref, out_ref):
-    state = before_ref[0]
-    for g in range(1, before_ref.shape[0]):
-        state = state + before_ref[g]
+    out_ref[...] = total
+
+
+def prefix_body(place_ref, part_ref, inner_ref, other_ref, *refs):
+    del inner_ref
+    *total_refs, out_ref = refs
+    place = place_ref[0]
+    state = jnp.where(place % 2 == 1, other_ref[...], 0.0)
+    for pair, total_ref in enumerate(total_refs, 1):
+        state = state + jnp.where((place // 2) ^ pair < place // 2, total_ref[...], 0.0)
     for m in range(part_ref.shape[0]):
         out_ref[m] = state
         if m + 1 < part_ref.shape[0]:
@@ -180,24 +182,29 @@
     )(query, key_in, value, gate, gain.reshape(1, width))
     parts, queries, inner, scale = lax.optimization_barrier((parts, queries, inner, scale))
 
+    def swap(a, bits):
+        return lax.ppermute(a, "grp", [(g, g ^ bits) for g in range(ranges)])
+
     place = lax.axis_index("grp").astype(jnp.int32).reshape(1)
     range_total = pl.pallas_call(
         total_body,
-        in_specs=[pl.BlockSpec(memory_space=pltpu.SMEM), VMEM],
+        in_specs=[VMEM],
         out_specs=VMEM,
-        out_shape=jax.ShapeDtypeStruct((ranges, piece, HEAD_DIM), jnp.float32),
+        out_shape=jax.ShapeDtypeStruct((piece, HEAD_DIM), jnp.float32),
         compiler_params=params(16),
         name="range_total",
-    )(place, parts)
-    before = lax.all_to_all(range_total, "grp", 0, 0, tiled=True)
+    )(parts)
+    other = swap(range_total, 1)
+    both = range_total + other
+    totals = [swap(both, 2 * pair) for pair in range(1, ranges // 2)]
     states = pl.pallas_call(
         prefix_body,
-        in_specs=[VMEM, VMEM],
+        in_specs=[pl.BlockSpec(memory_space=pltpu.SMEM)] + [VMEM] * (3 + len(totals)),
         out_specs=VMEM,
         out_shape=jax.ShapeDtypeStruct(parts.shape, jnp.float32),
         compiler_params=params(16),
         name="prefix",
-    )(parts, before)
+    )(place, parts, inner, other, *totals)
     state = lax.all_to_all(states, "seq", 0, 0, tiled=True).reshape(width, HEAD_DIM)
 
     return pl.pallas_call(

time: 66.7 us -> 64.8 us (0.972)
  blocking collectives: 32.8 us -> 21.5 us
  waiting for transfers between devices: 10 us -> 15.4 us
  starting transfers between devices: 11.2 us -> 15.4 us
    all_to_all x1 -> x0, blocking collectives: 10.7 us -> none  [per_device(): before = lax.all_to_all(range_total, 'grp', 0, 0, tiled=True)]
    ppermute x0 -> x4, waiting for transfers between devices: none -> 5.33 us  [swap(): return lax.ppermute(a, 'grp', [(g, g ^ bits) for g in range(ranges)])]
    ppermute x0 -> x4, starting transfers between devices: none -> 4.18 us  [swap(): return lax.ppermute(a, 'grp', [(g, g ^ bits) for g in range(ranges)])]
  transfers between devices with their start and end apart: 1 -> 5, of which waited for: 1 -> 4; matrix products, arithmetic and copies ran while one was open for 0% -> 0% of each run, Pallas kernels for 8% -> 8%
where the time goes in v4:
time: 64.8 us; the launch traced here: 64.6 us
  blocking collectives  21.5 us (33%)
  starting transfers between devices  15.4 us (24%)
  waiting for transfers between devices  15.4 us (24%)
  Pallas kernels  9.98 us (15%)
  local copies, waits for them, and re-layouts  2.3 us (4%)
    all_to_all x1, blocking collectives, per_device(): lax.all_to_all(states, 'seq', 0, 0, tiled=True).reshape(width, HEAD_DIM)  21.5 us
    all_to_all x1, starting transfers between devices, per_device(): lax.all_to_all(total.reshape(inner_ranges, piece, HEAD_DIM), 'seq', 0, 0,...  11.2 us
    all_to_all x1, waiting for transfers between devices, per_device(): lax.all_to_all(total.reshape(inner_ranges, piece, HEAD_DIM), 'seq', 0, 0,...  10.1 us
    ppermute x4, waiting for transfers between devices, swap(): return lax.ppermute(a, 'grp', [(g, g ^ bits) for g in range(ranges)])  5.33 us
    pallas_call x1, Pallas kernels, per_device(): pl.pallas_call(intra_body, in_specs=[HBM, HBM, HBM, HBM, VMEM], out_specs...  5.25 us
    ppermute x4, starting transfers between devices, swap(): return lax.ppermute(a, 'grp', [(g, g ^ bits) for g in range(ranges)])  4.18 us
    pallas_call x1, Pallas kernels, per_device(): pl.pallas_call(kv_body, in_specs=[HBM, HBM], out_specs=HBM, out_shape=plt...  3.05 us
    unnamed x10, local copies, waits for them, and re-layouts  2.3 us
  transfers between devices with their start and end apart: 5, of which 4 were waited for; matrix products, arithmetic and copies ran while one was open for 0% of the time, Pallas kernels for 8%

profile of v4, /device:TPU:32, one launch (start us, length us, event | category | flops | bytes accessed | tf_op | source)
XLA Modules:
  0.0 64.6 jit_solution(6052079911321932397)
XLA Ops:
  0.0 0.0 copy-start.4
  0.0 3.0 %range_part.1 = f32[1024,128]{1,0:T(8,128)} custom-call(bf16[512,1024]{1,0:T(8,128)(2,1)} %key_hbm.3, bf16[512,1024]{1,0:T(8,128)(2,1)} %value_hbm.3), custom_call_target="tpu_custom_call" | custom-call | tf_op jit(solution)/shard_map/range_part/pallas_call | solution.py:156
  3.1 11.2 %all-to-all-start = ((f32[32,32,128]{2,1,0:T(8,128)}), f32[32,32,128]{2,1,0:T(8,128)S(1)}, u32[]{:S(2)}, u32[]{:S(2)}) async-start(f32[32,32,128]{2,1,0:T(8,128)} %bitcast.6), calls=%async_computation | async-start | bytes 1048576 | tf_op jit(solution)/shard_map/all_to_all | solution.py:168
  14.3 0.0 copy-done.4
  14.3 5.2 %within_block.1 = (bf16[512,1024]{1,0:T(8,128)(2,1)S(1)}, f32[512,1024]{1,0:T(8,128)S(1)}, f32[512,1024]{1,0:T(8,128)S(1)}) custom-call(bf16[512,1024]{1,0:T(8,128)(2,1)} %query_hbm.1, bf16[512,1024]{1,0:T(8,128)(2,1)} %key_hbm.3, bf16[512,1024]{1,0:T(8,128)(2,1)} %value_hbm.3, bf16[512,1024]{1,0:T(8,128)(2,1)} %gate_hbm.1, f32[1,1024]{1,0:T(1,128)S(1)} %bitcast.5), custom_call_target="tpu_custom_call" | custom-call | tf_op jit(solution)/shard_map/within_block/pallas_call | solution.py:170
  19.5 0.0 copy-start
  19.5 1.3 %copy-done = f32[512,1024]{1,0:T(8,128)} copy-done((f32[512,1024]{1,0:T(8,128)}, f32[512,1024]{1,0:T(8,128)S(1)}, u32[]{:S(2)}) %copy-start) | copy-done | bytes 2097176
  20.9 0.0 copy-start.2
  20.9 1.0 %copy-done.2 = bf16[512,1024]{1,0:T(8,128)(2,1)} copy-done((bf16[512,1024]{1,0:T(8,128)(2,1)}, bf16[512,1024]{1,0:T(8,128)(2,1)S(1)}, u32[]{:S(2)}) %copy-start.2) | copy-done | bytes 1048600
  21.8 10.1 %all-to-all-done.part_ref = f32[32,32,128]{2,1,0:T(8,128)S(1)} async-done(((f32[32,32,128]{2,1,0:T(8,128)}), f32[32,32,128]{2,1,0:T(8,128)S(1)}, u32[]{:S(2)}, u32[]{:S(2)}) %all-to-all-start) | async-done | bytes 524320 | tf_op jit(solution)/shard_map/all_to_all | solution.py:168
  31.9 0.1 collective-permute-start
  32.0 1.2 %collective-permute-done.other_ref = f32[32,128]{1,0:T(8,128)S(1)} collective-permute-done((f32[32,128]{1,0:T(8,128)S(1)}, f32[32,128]{1,0:T(8,128)S(1)}, u32[]{:S(2)}, u32[]{:S(2)}) %collective-permute-start) | collective-permute-done | bytes 16416 | tf_op jit(solution)/shard_map/ppermute | solution.py:186
  33.2 3.0 %collective-permute-start.3 = (f32[32,128]{1,0:T(8,128)S(1)}, f32[32,128]{1,0:T(8,128)S(1)}, u32[]{:S(2)}, u32[]{:S(2)}) collective-permute-start(f32[32,128]{1,0:T(8,128)S(1)} %add.3), channel_id=1, source_target_pairs={{0,192},{32,224},{64,128},{96,160},{128,64},{160,96},{192,0},{224,... | collective-permute-start | bytes 49160 | tf_op jit(solution)/shard_map/ppermute | solution.py:186
  36.2 0.6 collective-permute-start.2
  36.8 0.5 collective-permute-start.1
  37.3 0.9 %collective-permute-done.3.refs_2_ = f32[32,128]{1,0:T(8,128)S(1)} collective-permute-done((f32[32,128]{1,0:T(8,128)S(1)}, f32[32,128]{1,0:T(8,128)S(1)}, u32[]{:S(2)}, u32[]{:S(2)}) %collective-permute-start.3) | collective-permute-done | bytes 16416 | tf_op jit(solution)/shard_map/ppermute | solution.py:186
  38.2 3.3 %collective-permute-done.2.refs_1_ = f32[32,128]{1,0:T(8,128)S(1)} collective-permute-done((f32[32,128]{1,0:T(8,128)S(1)}, f32[32,128]{1,0:T(8,128)S(1)}, u32[]{:S(2)}, u32[]{:S(2)}) %collective-permute-start.2) | collective-permute-done | bytes 16416 | tf_op jit(solution)/shard_map/ppermute | solution.py:186
  41.5 0.0 collective-permute-done.1.refs_0_
  41.5 0.0 copy-start.1
  41.5 0.0 copy-start.3
  41.5 21.5 %all_to_all.10 = f32[32,32,128]{2,1,0:T(8,128)S(1)} all-to-all(f32[32,32,128]{2,1,0:T(8,128)S(1)} %prefix.1), channel_id=1, replica_groups=mesh['grp'=8,'seq'=32] {'seq'}, dimensions={0} | all-to-all | bytes 1048576 | tf_op jit(solution)/shard_map/all_to_all | solution.py:208
  63.0 0.0 copy-done.1
  63.0 0.0 copy-done.3
  63.0 1.6 %gated_norm.1 = bf16[512,1024]{1,0:T(8,128)(2,1)} custom-call(bf16[512,1024]{1,0:T(8,128)(2,1)S(1)} %copy-done.3, f32[512,1024]{1,0:T(8,128)S(1)} %get-tuple-element.16.inner_ref, f32[512,1024]{1,0:T(8,128)S(1)} %copy-done.1, f32[1024,128]{1,0:T(8,128)S(1)} %bitcast.4), custom_call_target="tpu_custom_call" | custom-call | tf_op jit(solution)/shard_map/gated_norm/pallas_call | solution.py:210
  (3 shorter events, 0.1 us)
Async XLA Ops:
  0.0 14.3 %copy-start.4 = (f32[1024]{0:T(1024)S(1)}, f32[1024]{0:T(1024)}, u32[]{:S(2)}) copy-start(f32[1024]{0:T(1024)} %param.9) | copy-start | bytes 12292
  3.1 28.8 %all-to-all-start = ((f32[32,32,128]{2,1,0:T(8,128)}), f32[32,32,128]{2,1,0:T(8,128)S(1)}, u32[]{:S(2)}, u32[]{:S(2)}) async-start(f32[32,32,128]{2,1,0:T(8,128)} %bitcast.6), calls=%async_computation | async-start | bytes 1048576 | tf_op jit(solution)/shard_map/all_to_all | solution.py:168
  19.5 1.3 %copy-start = (f32[512,1024]{1,0:T(8,128)}, f32[512,1024]{1,0:T(8,128)S(1)}, u32[]{:S(2)}) copy-start(f32[512,1024]{1,0:T(8,128)S(1)} %get-tuple-element.17.scale_ref) | copy-start | bytes 6291460
  20.9 1.0 %copy-start.2 = (bf16[512,1024]{1,0:T(8,128)(2,1)}, bf16[512,1024]{1,0:T(8,128)(2,1)S(1)}, u32[]{:S(2)}) copy-start(bf16[512,1024]{1,0:T(8,128)(2,1)S(1)} %get-tuple-element.15.queries_ref) | copy-start | bytes 3145732
  31.9 1.3 %collective-permute-start = (f32[32,128]{1,0:T(8,128)S(1)}, f32[32,128]{1,0:T(8,128)S(1)}, u32[]{:S(2)}, u32[]{:S(2)}) collective-permute-start(f32[32,128]{1,0:T(8,128)S(1)} %range_total.1), channel_id=1, source_target_pairs={{0,32},{32,0},{64,96},{96,64},{128,160},{160,128},{192,224},{224,1... | collective-permute-start | bytes 49160 | tf_op jit(solution)/shard_map/ppermute | solution.py:186
  33.2 4.9 %collective-permute-start.3 = (f32[32,128]{1,0:T(8,128)S(1)}, f32[32,128]{1,0:T(8,128)S(1)}, u32[]{:S(2)}, u32[]{:S(2)}) collective-permute-start(f32[32,128]{1,0:T(8,128)S(1)} %add.3), channel_id=1, source_target_pairs={{0,192},{32,224},{64,128},{96,160},{128,64},{160,96},{192,0},{224,... | collective-permute-start | bytes 49160 | tf_op jit(solution)/shard_map/ppermute | solution.py:186
  36.2 5.2 %collective-permute-start.2 = (f32[32,128]{1,0:T(8,128)S(1)}, f32[32,128]{1,0:T(8,128)S(1)}, u32[]{:S(2)}, u32[]{:S(2)}) collective-permute-start(f32[32,128]{1,0:T(8,128)S(1)} %add.3), channel_id=1, source_target_pairs={{0,128},{32,160},{64,192},{96,224},{128,0},{160,32},{192,64},{224,... | collective-permute-start | bytes 49160 | tf_op jit(solution)/shard_map/ppermute | solution.py:186
  36.8 4.6 %collective-permute-start.1 = (f32[32,128]{1,0:T(8,128)S(1)}, f32[32,128]{1,0:T(8,128)S(1)}, u32[]{:S(2)}, u32[]{:S(2)}) collective-permute-start(f32[32,128]{1,0:T(8,128)S(1)} %add.3), channel_id=1, source_target_pairs={{0,64},{32,96},{64,0},{96,32},{128,192},{160,224},{192,128},{224,1... | collective-permute-start | bytes 49160 | tf_op jit(solution)/shard_map/ppermute | solution.py:186
  41.5 21.5 %copy-start.1 = (f32[512,1024]{1,0:T(8,128)S(1)}, f32[512,1024]{1,0:T(8,128)}, u32[]{:S(2)}) copy-start(f32[512,1024]{1,0:T(8,128)} %copy-done) | copy-start | bytes 6291460
  41.5 21.5 %copy-start.3 = (bf16[512,1024]{1,0:T(8,128)(2,1)S(1)}, bf16[512,1024]{1,0:T(8,128)(2,1)}, u32[]{:S(2)}) copy-start(bf16[512,1024]{1,0:T(8,128)(2,1)} %copy-done.2) | copy-start | bytes 3145732

commit v5 on v4

--- a/solution.py
+++ b/solution.py
@@ -1,10 +1,12 @@
 import functools
+import itertools
 
 import jax
 import jax.numpy as jnp
 from jax import lax
 from jax.experimental import pallas as pl
 from jax.experimental.pallas import tpu as pltpu
+from jax.sharding import Mesh
 from jax.sharding import PartitionSpec as P
 
 HEADS = 8
@@ -12,6 +14,7 @@
 BLOCK = 256
 LANES = 2 * HEAD_DIM
 KV_LANES = 4 * HEAD_DIM
+EXCHANGE_BITS = (0, 4, 3, 2, 1)
 
 
 def silu(u):
@@ -125,16 +128,16 @@
     out_ref[...] = total
 
 
-def prefix_body(place_ref, part_ref, inner_ref, other_ref, *refs):
+def prefix_body(order, place_ref, part_ref, inner_ref, other_ref, *refs):
     del inner_ref
     *total_refs, out_ref = refs
     place = place_ref[0]
     state = jnp.where(place % 2 == 1, other_ref[...], 0.0)
     for pair, total_ref in enumerate(total_refs, 1):
         state = state + jnp.where((place // 2) ^ pair < place // 2, total_ref[...], 0.0)
-    for m in range(part_ref.shape[0]):
+    for m in order:
         out_ref[m] = state
-        if m + 1 < part_ref.shape[0]:
+        if m != order[-1]:
             state = state + part_ref[m]
 
 
@@ -146,7 +149,7 @@
     return pltpu.CompilerParams(vmem_limit_bytes=mib * 1024 * 1024)
 
 
-def per_device(query, key_in, value, gate, gain, ranges, inner_ranges):
+def per_device(query, key_in, value, gate, gain, ranges, inner_ranges, exchange, order):
     rows, width = query.shape
     steps = width // LANES
     tokens = pltpu.VMEM((rows, width), jnp.bfloat16)
@@ -165,7 +168,7 @@
     )(key_in, value)
 
     piece = width // inner_ranges
-    parts = lax.all_to_all(total.reshape(inner_ranges, piece, HEAD_DIM), "seq", 0, 0, tiled=True)
+    parts = lax.all_to_all(total.reshape(inner_ranges, piece, HEAD_DIM), exchange, 0, 0, tiled=True)
 
     queries, inner, scale = pl.pallas_call(
         intra_body,
@@ -198,14 +201,14 @@
     both = range_total + other
     totals = [swap(both, 2 * pair) for pair in range(1, ranges // 2)]
     states = pl.pallas_call(
-        prefix_body,
+        functools.partial(prefix_body, order),
         in_specs=[pl.BlockSpec(memory_space=pltpu.SMEM)] + [VMEM] * (3 + len(totals)),
         out_specs=VMEM,
         out_shape=jax.ShapeDtypeStruct(parts.shape, jnp.float32),
         compiler_params=params(16),
         name="prefix",
     )(place, parts, inner, other, *totals)
-    state = lax.all_to_all(states, "seq", 0, 0, tiled=True).reshape(width, HEAD_DIM)
+    state = lax.all_to_all(states, exchange, 0, 0, tiled=True).reshape(width, HEAD_DIM)
 
     return pl.pallas_call(
         final_body,
@@ -219,16 +222,22 @@
 
 
 def solution(mesh):
+    ranges, inner_ranges = mesh.shape["grp"], mesh.shape["seq"]
+    bits = inner_ranges.bit_length() - 1
+    names = tuple(f"seq{b}" for b in reversed(range(bits)))
+    split = Mesh(mesh.devices.reshape((ranges,) + (2,) * bits), ("grp",) + names)
+    exchange = tuple(f"seq{b}" for b in EXCHANGE_BITS)
+    order = []
+    for index in itertools.product(range(2), repeat=bits):
+        bit = dict(zip(names, index))
+        order.append(sum(bit[name] << (bits - 1 - i) for i, name in enumerate(exchange)))
+    rows = P(("grp",) + names, None)
     return jax.shard_map(
-        functools.partial(per_device, ranges=mesh.shape["grp"], inner_ranges=mesh.shape["seq"]),
-        mesh=mesh,
-        in_specs=(
-            P(("grp", "seq"), None),
-            P(("grp", "seq"), None),
-            P(("grp", "seq"), None),
-            P(("grp", "seq"), None),
-            P(),
+        functools.partial(
+            per_device, ranges=ranges, inner_ranges=inner_ranges, exchange=exchange, order=tuple(order)
         ),
-        out_specs=P(("grp", "seq"), None),
+        mesh=split,
+        in_specs=(rows, rows, rows, rows, P()),
+        out_specs=rows,
         check_vma=False,
     )

time: 64.8 us -> 63.7 us (0.983); the launches traced: 64.6 us -> 62.7 us
  waiting for transfers between devices: 15.4 us -> 14 us
    all_to_all x1, waiting for transfers between devices: 10.1 us -> 8.64 us  [per_device(): lax.all_to_all(total.reshape(inner_ranges, piece, HEAD_DIM), exchange, 0,...]
where the time goes in v5:
time: 63.7 us; the launch traced here: 62.7 us
  blocking collectives  21 us (33%)
  starting transfers between devices  15.4 us (24%)
  waiting for transfers between devices  14 us (22%)
  Pallas kernels  9.98 us (16%)
  local copies, waits for them, and re-layouts  2.3 us (4%)
    all_to_all x1, blocking collectives, per_device(): lax.all_to_all(states, exchange, 0, 0, tiled=True).reshape(width, HEAD_DIM)  21 us
    all_to_all x1, starting transfers between devices, per_device(): lax.all_to_all(total.reshape(inner_ranges, piece, HEAD_DIM), exchange, 0,...  11.2 us
    all_to_all x1, waiting for transfers between devices, per_device(): lax.all_to_all(total.reshape(inner_ranges, piece, HEAD_DIM), exchange, 0,...  8.64 us
    ppermute x4, waiting for transfers between devices, swap(): return lax.ppermute(a, 'grp', [(g, g ^ bits) for g in range(ranges)])  5.34 us
    pallas_call x1, Pallas kernels, per_device(): pl.pallas_call(intra_body, in_specs=[HBM, HBM, HBM, HBM, VMEM], out_specs...  5.25 us
    ppermute x4, starting transfers between devices, swap(): return lax.ppermute(a, 'grp', [(g, g ^ bits) for g in range(ranges)])  4.18 us
    pallas_call x1, Pallas kernels, per_device(): pl.pallas_call(kv_body, in_specs=[HBM, HBM], out_specs=HBM, out_shape=plt...  3.05 us
    unnamed x10, local copies, waits for them, and re-layouts  2.3 us
  transfers between devices with their start and end apart: 5, of which 4 were waited for; matrix products, arithmetic and copies ran while one was open for 0% of the time, Pallas kernels for 8%

profile of v5, /device:TPU:32, one launch (start us, length us, event | category | flops | bytes accessed | tf_op | source)
XLA Modules:
  0.0 62.7 jit_solution(12124962782175473259)
XLA Ops:
  0.0 0.0 copy-start.4
  0.0 3.0 %range_part.1 = f32[1024,128]{1,0:T(8,128)} custom-call(bf16[512,1024]{1,0:T(8,128)(2,1)} %key_hbm.3, bf16[512,1024]{1,0:T(8,128)(2,1)} %value_hbm.3), custom_call_target="tpu_custom_call" | custom-call | tf_op jit(solution)/shard_map/range_part/pallas_call | solution.py:159
  3.1 11.2 %all-to-all-start = ((f32[32,32,128]{2,1,0:T(8,128)}), f32[32,32,128]{2,1,0:T(8,128)S(1)}, u32[]{:S(2)}, u32[]{:S(2)}) async-start(f32[32,32,128]{2,1,0:T(8,128)} %bitcast.6), calls=%async_computation | async-start | bytes 1048576 | tf_op jit(solution)/shard_map/all_to_all | solution.py:171
  14.3 0.0 copy-done.4
  14.3 5.2 %within_block.1 = (bf16[512,1024]{1,0:T(8,128)(2,1)S(1)}, f32[512,1024]{1,0:T(8,128)S(1)}, f32[512,1024]{1,0:T(8,128)S(1)}) custom-call(bf16[512,1024]{1,0:T(8,128)(2,1)} %query_hbm.1, bf16[512,1024]{1,0:T(8,128)(2,1)} %key_hbm.3, bf16[512,1024]{1,0:T(8,128)(2,1)} %value_hbm.3, bf16[512,1024]{1,0:T(8,128)(2,1)} %gate_hbm.1, f32[1,1024]{1,0:T(1,128)S(1)} %bitcast.5), custom_call_target="tpu_custom_call" | custom-call | tf_op jit(solution)/shard_map/within_block/pallas_call | solution.py:173
  19.5 0.0 copy-start
  19.6 1.3 %copy-done = f32[512,1024]{1,0:T(8,128)} copy-done((f32[512,1024]{1,0:T(8,128)}, f32[512,1024]{1,0:T(8,128)S(1)}, u32[]{:S(2)}) %copy-start) | copy-done | bytes 2097176
  20.9 0.0 copy-start.2
  20.9 1.0 %copy-done.2 = bf16[512,1024]{1,0:T(8,128)(2,1)} copy-done((bf16[512,1024]{1,0:T(8,128)(2,1)}, bf16[512,1024]{1,0:T(8,128)(2,1)S(1)}, u32[]{:S(2)}) %copy-start.2) | copy-done | bytes 1048600
  21.8 8.6 %all-to-all-done.part_ref = f32[32,32,128]{2,1,0:T(8,128)S(1)} async-done(((f32[32,32,128]{2,1,0:T(8,128)}), f32[32,32,128]{2,1,0:T(8,128)S(1)}, u32[]{:S(2)}, u32[]{:S(2)}) %all-to-all-start) | async-done | bytes 524320 | tf_op jit(solution)/shard_map/all_to_all | solution.py:171
  30.5 0.1 collective-permute-start
  30.6 1.2 %collective-permute-done.other_ref = f32[32,128]{1,0:T(8,128)S(1)} collective-permute-done((f32[32,128]{1,0:T(8,128)S(1)}, f32[32,128]{1,0:T(8,128)S(1)}, u32[]{:S(2)}, u32[]{:S(2)}) %collective-permute-start) | collective-permute-done | bytes 16416 | tf_op jit(solution)/shard_map/ppermute | solution.py:189
  31.8 3.0 %collective-permute-start.3 = (f32[32,128]{1,0:T(8,128)S(1)}, f32[32,128]{1,0:T(8,128)S(1)}, u32[]{:S(2)}, u32[]{:S(2)}) collective-permute-start(f32[32,128]{1,0:T(8,128)S(1)} %add.3), channel_id=1, source_target_pairs={{0,192},{32,224},{64,128},{96,160},{128,64},{160,96},{192,0},{224,... | collective-permute-start | bytes 49160 | tf_op jit(solution)/shard_map/ppermute | solution.py:189
  34.8 0.6 %collective-permute-start.2 = (f32[32,128]{1,0:T(8,128)S(1)}, f32[32,128]{1,0:T(8,128)S(1)}, u32[]{:S(2)}, u32[]{:S(2)}) collective-permute-start(f32[32,128]{1,0:T(8,128)S(1)} %add.3), channel_id=1, source_target_pairs={{0,128},{32,160},{64,192},{96,224},{128,0},{160,32},{192,64},{224,... | collective-permute-start | bytes 49160 | tf_op jit(solution)/shard_map/ppermute | solution.py:189
  35.4 0.4 collective-permute-start.1
  35.9 0.9 %collective-permute-done.3.refs_2_ = f32[32,128]{1,0:T(8,128)S(1)} collective-permute-done((f32[32,128]{1,0:T(8,128)S(1)}, f32[32,128]{1,0:T(8,128)S(1)}, u32[]{:S(2)}, u32[]{:S(2)}) %collective-permute-start.3) | collective-permute-done | bytes 16416 | tf_op jit(solution)/shard_map/ppermute | solution.py:189
  36.8 3.3 %collective-permute-done.2.refs_1_ = f32[32,128]{1,0:T(8,128)S(1)} collective-permute-done((f32[32,128]{1,0:T(8,128)S(1)}, f32[32,128]{1,0:T(8,128)S(1)}, u32[]{:S(2)}, u32[]{:S(2)}) %collective-permute-start.2) | collective-permute-done | bytes 16416 | tf_op jit(solution)/shard_map/ppermute | solution.py:189
  40.1 0.0 collective-permute-done.1.refs_0_
  40.1 0.0 copy-start.1
  40.1 0.0 copy-start.3
  40.1 21.0 %all_to_all.10 = f32[32,32,128]{2,1,0:T(8,128)S(1)} all-to-all(f32[32,32,128]{2,1,0:T(8,128)S(1)} %prefix.1), channel_id=1, replica_groups=mesh['grp'=8,'seq4'=2,'seq3'=2,'seq2'=2,'seq1'=2,'seq0'=2] {'seq0','seq4..., dimensions={0} | all-to-all | bytes 1048576 | tf_op jit(solution)/shard_map/all_to_all | solution.py:211
  61.1 0.0 copy-done.1
  61.1 0.0 copy-done.3
  61.1 1.6 %gated_norm.1 = bf16[512,1024]{1,0:T(8,128)(2,1)} custom-call(bf16[512,1024]{1,0:T(8,128)(2,1)S(1)} %copy-done.3, f32[512,1024]{1,0:T(8,128)S(1)} %get-tuple-element.16.inner_ref, f32[512,1024]{1,0:T(8,128)S(1)} %copy-done.1, f32[1024,128]{1,0:T(8,128)S(1)} %bitcast.4), custom_call_target="tpu_custom_call" | custom-call | tf_op jit(solution)/shard_map/gated_norm/pallas_call | solution.py:213
  (3 shorter events, 0.1 us)
Async XLA Ops:
  0.0 14.3 %copy-start.4 = (f32[1024]{0:T(1024)S(1)}, f32[1024]{0:T(1024)}, u32[]{:S(2)}) copy-start(f32[1024]{0:T(1024)} %param.9) | copy-start | bytes 12292
  3.1 27.4 %all-to-all-start = ((f32[32,32,128]{2,1,0:T(8,128)}), f32[32,32,128]{2,1,0:T(8,128)S(1)}, u32[]{:S(2)}, u32[]{:S(2)}) async-start(f32[32,32,128]{2,1,0:T(8,128)} %bitcast.6), calls=%async_computation | async-start | bytes 1048576 | tf_op jit(solution)/shard_map/all_to_all | solution.py:171
  19.5 1.3 %copy-start = (f32[512,1024]{1,0:T(8,128)}, f32[512,1024]{1,0:T(8,128)S(1)}, u32[]{:S(2)}) copy-start(f32[512,1024]{1,0:T(8,128)S(1)} %get-tuple-element.17.scale_ref) | copy-start | bytes 6291460
  20.9 1.0 %copy-start.2 = (bf16[512,1024]{1,0:T(8,128)(2,1)}, bf16[512,1024]{1,0:T(8,128)(2,1)S(1)}, u32[]{:S(2)}) copy-start(bf16[512,1024]{1,0:T(8,128)(2,1)S(1)} %get-tuple-element.15.queries_ref) | copy-start | bytes 3145732
  30.5 1.3 %collective-permute-start = (f32[32,128]{1,0:T(8,128)S(1)}, f32[32,128]{1,0:T(8,128)S(1)}, u32[]{:S(2)}, u32[]{:S(2)}) collective-permute-start(f32[32,128]{1,0:T(8,128)S(1)} %range_total.1), channel_id=1, source_target_pairs={{0,32},{32,0},{64,96},{96,64},{128,160},{160,128},{192,224},{224,1... | collective-permute-start | bytes 49160 | tf_op jit(solution)/shard_map/ppermute | solution.py:189
  31.8 4.9 %collective-permute-start.3 = (f32[32,128]{1,0:T(8,128)S(1)}, f32[32,128]{1,0:T(8,128)S(1)}, u32[]{:S(2)}, u32[]{:S(2)}) collective-permute-start(f32[32,128]{1,0:T(8,128)S(1)} %add.3), channel_id=1, source_target_pairs={{0,192},{32,224},{64,128},{96,160},{128,64},{160,96},{192,0},{224,... | collective-permute-start | bytes 49160 | tf_op jit(solution)/shard_map/ppermute | solution.py:189
  34.8 5.2 %collective-permute-start.2 = (f32[32,128]{1,0:T(8,128)S(1)}, f32[32,128]{1,0:T(8,128)S(1)}, u32[]{:S(2)}, u32[]{:S(2)}) collective-permute-start(f32[32,128]{1,0:T(8,128)S(1)} %add.3), channel_id=1, source_target_pairs={{0,128},{32,160},{64,192},{96,224},{128,0},{160,32},{192,64},{224,... | collective-permute-start | bytes 49160 | tf_op jit(solution)/shard_map/ppermute | solution.py:189
  35.4 4.6 %collective-permute-start.1 = (f32[32,128]{1,0:T(8,128)S(1)}, f32[32,128]{1,0:T(8,128)S(1)}, u32[]{:S(2)}, u32[]{:S(2)}) collective-permute-start(f32[32,128]{1,0:T(8,128)S(1)} %add.3), channel_id=1, source_target_pairs={{0,64},{32,96},{64,0},{96,32},{128,192},{160,224},{192,128},{224,1... | collective-permute-start | bytes 49160 | tf_op jit(solution)/shard_map/ppermute | solution.py:189
  40.1 21.1 %copy-start.1 = (f32[512,1024]{1,0:T(8,128)S(1)}, f32[512,1024]{1,0:T(8,128)}, u32[]{:S(2)}) copy-start(f32[512,1024]{1,0:T(8,128)} %copy-done) | copy-start | bytes 6291460
  40.1 21.1 %copy-start.3 = (bf16[512,1024]{1,0:T(8,128)(2,1)S(1)}, bf16[512,1024]{1,0:T(8,128)(2,1)}, u32[]{:S(2)}) copy-start(bf16[512,1024]{1,0:T(8,128)(2,1)} %copy-done.2) | copy-start | bytes 3145732

commit v6 on v5

--- a/solution.py
+++ b/solution.py
@@ -18,8 +18,8 @@
 
 
 def silu(u):
-    u = u.astype(jnp.float32)
-    return (u / (1.0 + jnp.exp(-u))).astype(jnp.bfloat16)
+    half = 0.5 * u.astype(jnp.float32)
+    return (half + half * jnp.tanh(half)).astype(jnp.bfloat16)
 
 
 def dot(a, b, contract):

time: 63.7 us -> 63.5 us (level)
  no operation moved by 1% of the time
where the time goes in v6:
time: 63.5 us; the launch traced here: 62.6 us
  blocking collectives  21 us (33%)
  starting transfers between devices  15.4 us (24%)
  waiting for transfers between devices  14 us (22%)
  Pallas kernels  9.82 us (15%)
  local copies, waits for them, and re-layouts  2.3 us (4%)
    all_to_all x1, blocking collectives, per_device(): lax.all_to_all(states, exchange, 0, 0, tiled=True).reshape(width, HEAD_DIM)  21 us
    all_to_all x1, starting transfers between devices, per_device(): lax.all_to_all(total.reshape(inner_ranges, piece, HEAD_DIM), exchange, 0,...  11.2 us
    all_to_all x1, waiting for transfers between devices, per_device(): lax.all_to_all(total.reshape(inner_ranges, piece, HEAD_DIM), exchange, 0,...  8.65 us
    ppermute x4, waiting for transfers between devices, swap(): return lax.ppermute(a, 'grp', [(g, g ^ bits) for g in range(ranges)])  5.33 us
    pallas_call x1, Pallas kernels, per_device(): pl.pallas_call(intra_body, in_specs=[HBM, HBM, HBM, HBM, VMEM], out_specs...  5.24 us
    ppermute x4, starting transfers between devices, swap(): return lax.ppermute(a, 'grp', [(g, g ^ bits) for g in range(ranges)])  4.18 us
    pallas_call x1, Pallas kernels, per_device(): pl.pallas_call(kv_body, in_specs=[HBM, HBM], out_specs=HBM, out_shape=plt...  2.89 us
    unnamed x10, local copies, waits for them, and re-layouts  2.3 us
  transfers between devices with their start and end apart: 5, of which 4 were waited for; matrix products, arithmetic and copies ran while one was open for 0% of the time, Pallas kernels for 8%

profile of v6, /device:TPU:32, one launch (start us, length us, event | category | flops | bytes accessed | tf_op | source)
XLA Modules:
  0.0 62.6 jit_solution(13171073872602368442)
XLA Ops:
  0.0 0.0 copy-start.4
  0.0 2.9 %range_part.1 = f32[1024,128]{1,0:T(8,128)} custom-call(bf16[512,1024]{1,0:T(8,128)(2,1)} %key_hbm.3, bf16[512,1024]{1,0:T(8,128)(2,1)} %value_hbm.3), custom_call_target="tpu_custom_call" | custom-call | tf_op jit(solution)/shard_map/range_part/pallas_call | solution.py:159
  2.9 11.2 %all-to-all-start = ((f32[32,32,128]{2,1,0:T(8,128)}), f32[32,32,128]{2,1,0:T(8,128)S(1)}, u32[]{:S(2)}, u32[]{:S(2)}) async-start(f32[32,32,128]{2,1,0:T(8,128)} %bitcast.6), calls=%async_computation | async-start | bytes 1048576 | tf_op jit(solution)/shard_map/all_to_all | solution.py:171
  14.1 0.0 copy-done.4
  14.1 5.2 %within_block.1 = (bf16[512,1024]{1,0:T(8,128)(2,1)S(1)}, f32[512,1024]{1,0:T(8,128)S(1)}, f32[512,1024]{1,0:T(8,128)S(1)}) custom-call(bf16[512,1024]{1,0:T(8,128)(2,1)} %query_hbm.1, bf16[512,1024]{1,0:T(8,128)(2,1)} %key_hbm.3, bf16[512,1024]{1,0:T(8,128)(2,1)} %value_hbm.3, bf16[512,1024]{1,0:T(8,128)(2,1)} %gate_hbm.1, f32[1,1024]{1,0:T(1,128)S(1)} %bitcast.5), custom_call_target="tpu_custom_call" | custom-call | tf_op jit(solution)/shard_map/within_block/pallas_call | solution.py:173
  19.4 0.0 copy-start
  19.4 1.3 %copy-done = f32[512,1024]{1,0:T(8,128)} copy-done((f32[512,1024]{1,0:T(8,128)}, f32[512,1024]{1,0:T(8,128)S(1)}, u32[]{:S(2)}) %copy-start) | copy-done | bytes 2097176
  20.7 0.0 copy-start.2
  20.7 1.0 %copy-done.2 = bf16[512,1024]{1,0:T(8,128)(2,1)} copy-done((bf16[512,1024]{1,0:T(8,128)(2,1)}, bf16[512,1024]{1,0:T(8,128)(2,1)S(1)}, u32[]{:S(2)}) %copy-start.2) | copy-done | bytes 1048600
  21.7 8.7 %all-to-all-done.part_ref = f32[32,32,128]{2,1,0:T(8,128)S(1)} async-done(((f32[32,32,128]{2,1,0:T(8,128)}), f32[32,32,128]{2,1,0:T(8,128)S(1)}, u32[]{:S(2)}, u32[]{:S(2)}) %all-to-all-start) | async-done | bytes 524320 | tf_op jit(solution)/shard_map/all_to_all | solution.py:171
  30.4 0.1 collective-permute-start
  30.5 1.2 %collective-permute-done.other_ref = f32[32,128]{1,0:T(8,128)S(1)} collective-permute-done((f32[32,128]{1,0:T(8,128)S(1)}, f32[32,128]{1,0:T(8,128)S(1)}, u32[]{:S(2)}, u32[]{:S(2)}) %collective-permute-start) | collective-permute-done | bytes 16416 | tf_op jit(solution)/shard_map/ppermute | solution.py:189
  31.6 3.0 %collective-permute-start.3 = (f32[32,128]{1,0:T(8,128)S(1)}, f32[32,128]{1,0:T(8,128)S(1)}, u32[]{:S(2)}, u32[]{:S(2)}) collective-permute-start(f32[32,128]{1,0:T(8,128)S(1)} %add.3), channel_id=1, source_target_pairs={{0,192},{32,224},{64,128},{96,160},{128,64},{160,96},{192,0},{224,... | collective-permute-start | bytes 49160 | tf_op jit(solution)/shard_map/ppermute | solution.py:189
  34.7 0.6 %collective-permute-start.2 = (f32[32,128]{1,0:T(8,128)S(1)}, f32[32,128]{1,0:T(8,128)S(1)}, u32[]{:S(2)}, u32[]{:S(2)}) collective-permute-start(f32[32,128]{1,0:T(8,128)S(1)} %add.3), channel_id=1, source_target_pairs={{0,128},{32,160},{64,192},{96,224},{128,0},{160,32},{192,64},{224,... | collective-permute-start | bytes 49160 | tf_op jit(solution)/shard_map/ppermute | solution.py:189
  35.3 0.5 collective-permute-start.1
  35.7 0.9 %collective-permute-done.3.refs_2_ = f32[32,128]{1,0:T(8,128)S(1)} collective-permute-done((f32[32,128]{1,0:T(8,128)S(1)}, f32[32,128]{1,0:T(8,128)S(1)}, u32[]{:S(2)}, u32[]{:S(2)}) %collective-permute-start.3) | collective-permute-done | bytes 16416 | tf_op jit(solution)/shard_map/ppermute | solution.py:189
  36.6 3.3 %collective-permute-done.2.refs_1_ = f32[32,128]{1,0:T(8,128)S(1)} collective-permute-done((f32[32,128]{1,0:T(8,128)S(1)}, f32[32,128]{1,0:T(8,128)S(1)}, u32[]{:S(2)}, u32[]{:S(2)}) %collective-permute-start.2) | collective-permute-done | bytes 16416 | tf_op jit(solution)/shard_map/ppermute | solution.py:189
  39.9 0.0 collective-permute-done.1.refs_0_
  39.9 0.0 copy-start.1
  39.9 0.0 copy-start.3
  40.0 21.0 %all_to_all.10 = f32[32,32,128]{2,1,0:T(8,128)S(1)} all-to-all(f32[32,32,128]{2,1,0:T(8,128)S(1)} %prefix.1), channel_id=1, replica_groups=mesh['grp'=8,'seq4'=2,'seq3'=2,'seq2'=2,'seq1'=2,'seq0'=2] {'seq0','seq4..., dimensions={0} | all-to-all | bytes 1048576 | tf_op jit(solution)/shard_map/all_to_all | solution.py:211
  61.0 0.0 copy-done.1
  61.0 0.0 copy-done.3
  61.0 1.6 %gated_norm.1 = bf16[512,1024]{1,0:T(8,128)(2,1)} custom-call(bf16[512,1024]{1,0:T(8,128)(2,1)S(1)} %copy-done.3, f32[512,1024]{1,0:T(8,128)S(1)} %get-tuple-element.16.inner_ref, f32[512,1024]{1,0:T(8,128)S(1)} %copy-done.1, f32[1024,128]{1,0:T(8,128)S(1)} %bitcast.4), custom_call_target="tpu_custom_call" | custom-call | tf_op jit(solution)/shard_map/gated_norm/pallas_call | solution.py:213
  (3 shorter events, 0.1 us)
Async XLA Ops:
  0.0 14.1 %copy-start.4 = (f32[1024]{0:T(1024)S(1)}, f32[1024]{0:T(1024)}, u32[]{:S(2)}) copy-start(f32[1024]{0:T(1024)} %param.9) | copy-start | bytes 12292
  2.9 27.4 %all-to-all-start = ((f32[32,32,128]{2,1,0:T(8,128)}), f32[32,32,128]{2,1,0:T(8,128)S(1)}, u32[]{:S(2)}, u32[]{:S(2)}) async-start(f32[32,32,128]{2,1,0:T(8,128)} %bitcast.6), calls=%async_computation | async-start | bytes 1048576 | tf_op jit(solution)/shard_map/all_to_all | solution.py:171
  19.4 1.3 %copy-start = (f32[512,1024]{1,0:T(8,128)}, f32[512,1024]{1,0:T(8,128)S(1)}, u32[]{:S(2)}) copy-start(f32[512,1024]{1,0:T(8,128)S(1)} %get-tuple-element.17.scale_ref) | copy-start | bytes 6291460
  20.7 1.0 %copy-start.2 = (bf16[512,1024]{1,0:T(8,128)(2,1)}, bf16[512,1024]{1,0:T(8,128)(2,1)S(1)}, u32[]{:S(2)}) copy-start(bf16[512,1024]{1,0:T(8,128)(2,1)S(1)} %get-tuple-element.15.queries_ref) | copy-start | bytes 3145732
  30.4 1.3 %collective-permute-start = (f32[32,128]{1,0:T(8,128)S(1)}, f32[32,128]{1,0:T(8,128)S(1)}, u32[]{:S(2)}, u32[]{:S(2)}) collective-permute-start(f32[32,128]{1,0:T(8,128)S(1)} %range_total.1), channel_id=1, source_target_pairs={{0,32},{32,0},{64,96},{96,64},{128,160},{160,128},{192,224},{224,1... | collective-permute-start | bytes 49160 | tf_op jit(solution)/shard_map/ppermute | solution.py:189
  31.6 4.9 %collective-permute-start.3 = (f32[32,128]{1,0:T(8,128)S(1)}, f32[32,128]{1,0:T(8,128)S(1)}, u32[]{:S(2)}, u32[]{:S(2)}) collective-permute-start(f32[32,128]{1,0:T(8,128)S(1)} %add.3), channel_id=1, source_target_pairs={{0,192},{32,224},{64,128},{96,160},{128,64},{160,96},{192,0},{224,... | collective-permute-start | bytes 49160 | tf_op jit(solution)/shard_map/ppermute | solution.py:189
  34.7 5.2 %collective-permute-start.2 = (f32[32,128]{1,0:T(8,128)S(1)}, f32[32,128]{1,0:T(8,128)S(1)}, u32[]{:S(2)}, u32[]{:S(2)}) collective-permute-start(f32[32,128]{1,0:T(8,128)S(1)} %add.3), channel_id=1, source_target_pairs={{0,128},{32,160},{64,192},{96,224},{128,0},{160,32},{192,64},{224,... | collective-permute-start | bytes 49160 | tf_op jit(solution)/shard_map/ppermute | solution.py:189
  35.3 4.6 %collective-permute-start.1 = (f32[32,128]{1,0:T(8,128)S(1)}, f32[32,128]{1,0:T(8,128)S(1)}, u32[]{:S(2)}, u32[]{:S(2)}) collective-permute-start(f32[32,128]{1,0:T(8,128)S(1)} %add.3), channel_id=1, source_target_pairs={{0,64},{32,96},{64,0},{96,32},{128,192},{160,224},{192,128},{224,1... | collective-permute-start | bytes 49160 | tf_op jit(solution)/shard_map/ppermute | solution.py:189
  39.9 21.1 %copy-start.1 = (f32[512,1024]{1,0:T(8,128)S(1)}, f32[512,1024]{1,0:T(8,128)}, u32[]{:S(2)}) copy-start(f32[512,1024]{1,0:T(8,128)} %copy-done) | copy-start | bytes 6291460
  39.9 21.1 %copy-start.3 = (bf16[512,1024]{1,0:T(8,128)(2,1)S(1)}, bf16[512,1024]{1,0:T(8,128)(2,1)}, u32[]{:S(2)}) copy-start(bf16[512,1024]{1,0:T(8,128)(2,1)} %copy-done.2) | copy-start | bytes 3145732

commit v7 on v6

--- a/solution.py
+++ b/solution.py
@@ -14,7 +14,7 @@
 BLOCK = 256
 LANES = 2 * HEAD_DIM
 KV_LANES = 4 * HEAD_DIM
-EXCHANGE_BITS = (0, 4, 3, 2, 1)
+EXCHANGE_BITS = (0, 4, 2, 3, 1)
 
 
 def silu(u):

time: 63.5 us -> 63.6 us (level)
  no operation moved by 1% of the time
where the time goes in v7:
time: 63.6 us; the launch traced here: 62.7 us
  blocking collectives  21.2 us (33%)
  starting transfers between devices  15.4 us (24%)
  waiting for transfers between devices  14 us (22%)
  Pallas kernels  9.82 us (15%)
  local copies, waits for them, and re-layouts  2.3 us (4%)
    all_to_all x1, blocking collectives, per_device(): lax.all_to_all(states, exchange, 0, 0, tiled=True).reshape(width, HEAD_DIM)  21.2 us
    all_to_all x1, starting transfers between devices, per_device(): lax.all_to_all(total.reshape(inner_ranges, piece, HEAD_DIM), exchange, 0,...  11.2 us
    all_to_all x1, waiting for transfers between devices, per_device(): lax.all_to_all(total.reshape(inner_ranges, piece, HEAD_DIM), exchange, 0,...  8.64 us
    ppermute x4, waiting for transfers between devices, swap(): return lax.ppermute(a, 'grp', [(g, g ^ bits) for g in range(ranges)])  5.33 us
    pallas_call x1, Pallas kernels, per_device(): pl.pallas_call(intra_body, in_specs=[HBM, HBM, HBM, HBM, VMEM], out_specs...  5.24 us
    ppermute x4, starting transfers between devices, swap(): return lax.ppermute(a, 'grp', [(g, g ^ bits) for g in range(ranges)])  4.18 us
    pallas_call x1, Pallas kernels, per_device(): pl.pallas_call(kv_body, in_specs=[HBM, HBM], out_specs=HBM, out_shape=plt...  2.89 us
    unnamed x10, local copies, waits for them, and re-layouts  2.3 us
  transfers between devices with their start and end apart: 5, of which 4 were waited for; matrix products, arithmetic and copies ran while one was open for 0% of the time, Pallas kernels for 8%

profile of v7, /device:TPU:32, one launch (start us, length us, event | category | flops | bytes accessed | tf_op | source)
XLA Modules:
  0.0 62.7 jit_solution(13071895290754519083)
XLA Ops:
  0.0 0.0 copy-start.4
  0.0 2.9 %range_part.1 = f32[1024,128]{1,0:T(8,128)} custom-call(bf16[512,1024]{1,0:T(8,128)(2,1)} %key_hbm.3, bf16[512,1024]{1,0:T(8,128)(2,1)} %value_hbm.3), custom_call_target="tpu_custom_call" | custom-call | tf_op jit(solution)/shard_map/range_part/pallas_call | solution.py:159
  2.9 11.2 %all-to-all-start = ((f32[32,32,128]{2,1,0:T(8,128)}), f32[32,32,128]{2,1,0:T(8,128)S(1)}, u32[]{:S(2)}, u32[]{:S(2)}) async-start(f32[32,32,128]{2,1,0:T(8,128)} %bitcast.6), calls=%async_computation | async-start | bytes 1048576 | tf_op jit(solution)/shard_map/all_to_all | solution.py:171
  14.1 0.0 copy-done.4
  14.1 5.2 %within_block.1 = (bf16[512,1024]{1,0:T(8,128)(2,1)S(1)}, f32[512,1024]{1,0:T(8,128)S(1)}, f32[512,1024]{1,0:T(8,128)S(1)}) custom-call(bf16[512,1024]{1,0:T(8,128)(2,1)} %query_hbm.1, bf16[512,1024]{1,0:T(8,128)(2,1)} %key_hbm.3, bf16[512,1024]{1,0:T(8,128)(2,1)} %value_hbm.3, bf16[512,1024]{1,0:T(8,128)(2,1)} %gate_hbm.1, f32[1,1024]{1,0:T(1,128)S(1)} %bitcast.5), custom_call_target="tpu_custom_call" | custom-call | tf_op jit(solution)/shard_map/within_block/pallas_call | solution.py:173
  19.4 0.0 copy-start
  19.4 1.3 %copy-done = f32[512,1024]{1,0:T(8,128)} copy-done((f32[512,1024]{1,0:T(8,128)}, f32[512,1024]{1,0:T(8,128)S(1)}, u32[]{:S(2)}) %copy-start) | copy-done | bytes 2097176
  20.7 0.0 copy-start.2
  20.7 1.0 %copy-done.2 = bf16[512,1024]{1,0:T(8,128)(2,1)} copy-done((bf16[512,1024]{1,0:T(8,128)(2,1)}, bf16[512,1024]{1,0:T(8,128)(2,1)S(1)}, u32[]{:S(2)}) %copy-start.2) | copy-done | bytes 1048600
  21.7 8.6 %all-to-all-done.part_ref = f32[32,32,128]{2,1,0:T(8,128)S(1)} async-done(((f32[32,32,128]{2,1,0:T(8,128)}), f32[32,32,128]{2,1,0:T(8,128)S(1)}, u32[]{:S(2)}, u32[]{:S(2)}) %all-to-all-start) | async-done | bytes 524320 | tf_op jit(solution)/shard_map/all_to_all | solution.py:171
  30.4 0.1 collective-permute-start
  30.5 1.2 %collective-permute-done.other_ref = f32[32,128]{1,0:T(8,128)S(1)} collective-permute-done((f32[32,128]{1,0:T(8,128)S(1)}, f32[32,128]{1,0:T(8,128)S(1)}, u32[]{:S(2)}, u32[]{:S(2)}) %collective-permute-start) | collective-permute-done | bytes 16416 | tf_op jit(solution)/shard_map/ppermute | solution.py:189
  31.6 3.0 %collective-permute-start.3 = (f32[32,128]{1,0:T(8,128)S(1)}, f32[32,128]{1,0:T(8,128)S(1)}, u32[]{:S(2)}, u32[]{:S(2)}) collective-permute-start(f32[32,128]{1,0:T(8,128)S(1)} %add.3), channel_id=1, source_target_pairs={{0,192},{32,224},{64,128},{96,160},{128,64},{160,96},{192,0},{224,... | collective-permute-start | bytes 49160 | tf_op jit(solution)/shard_map/ppermute | solution.py:189
  34.6 0.6 %collective-permute-start.2 = (f32[32,128]{1,0:T(8,128)S(1)}, f32[32,128]{1,0:T(8,128)S(1)}, u32[]{:S(2)}, u32[]{:S(2)}) collective-permute-start(f32[32,128]{1,0:T(8,128)S(1)} %add.3), channel_id=1, source_target_pairs={{0,128},{32,160},{64,192},{96,224},{128,0},{160,32},{192,64},{224,... | collective-permute-start | bytes 49160 | tf_op jit(solution)/shard_map/ppermute | solution.py:189
  35.3 0.5 collective-permute-start.1
  35.7 0.9 %collective-permute-done.3.refs_2_ = f32[32,128]{1,0:T(8,128)S(1)} collective-permute-done((f32[32,128]{1,0:T(8,128)S(1)}, f32[32,128]{1,0:T(8,128)S(1)}, u32[]{:S(2)}, u32[]{:S(2)}) %collective-permute-start.3) | collective-permute-done | bytes 16416 | tf_op jit(solution)/shard_map/ppermute | solution.py:189
  36.6 3.3 %collective-permute-done.2.refs_1_ = f32[32,128]{1,0:T(8,128)S(1)} collective-permute-done((f32[32,128]{1,0:T(8,128)S(1)}, f32[32,128]{1,0:T(8,128)S(1)}, u32[]{:S(2)}, u32[]{:S(2)}) %collective-permute-start.2) | collective-permute-done | bytes 16416 | tf_op jit(solution)/shard_map/ppermute | solution.py:189
  39.9 0.0 collective-permute-done.1.refs_0_
  39.9 0.0 copy-start.1
  39.9 0.0 copy-start.3
  40.0 21.2 %all_to_all.10 = f32[32,32,128]{2,1,0:T(8,128)S(1)} all-to-all(f32[32,32,128]{2,1,0:T(8,128)S(1)} %prefix.1), channel_id=1, replica_groups=mesh['grp'=8,'seq4'=2,'seq3'=2,'seq2'=2,'seq1'=2,'seq0'=2] {'seq0','seq4..., dimensions={0} | all-to-all | bytes 1048576 | tf_op jit(solution)/shard_map/all_to_all | solution.py:211
  61.1 0.0 copy-done.1
  61.1 0.0 copy-done.3
  61.1 1.6 %gated_norm.1 = bf16[512,1024]{1,0:T(8,128)(2,1)} custom-call(bf16[512,1024]{1,0:T(8,128)(2,1)S(1)} %copy-done.3, f32[512,1024]{1,0:T(8,128)S(1)} %get-tuple-element.16.inner_ref, f32[512,1024]{1,0:T(8,128)S(1)} %copy-done.1, f32[1024,128]{1,0:T(8,128)S(1)} %bitcast.4), custom_call_target="tpu_custom_call" | custom-call | tf_op jit(solution)/shard_map/gated_norm/pallas_call | solution.py:213
  (3 shorter events, 0.1 us)
Async XLA Ops:
  0.0 14.1 %copy-start.4 = (f32[1024]{0:T(1024)S(1)}, f32[1024]{0:T(1024)}, u32[]{:S(2)}) copy-start(f32[1024]{0:T(1024)} %param.9) | copy-start | bytes 12292
  2.9 27.4 %all-to-all-start = ((f32[32,32,128]{2,1,0:T(8,128)}), f32[32,32,128]{2,1,0:T(8,128)S(1)}, u32[]{:S(2)}, u32[]{:S(2)}) async-start(f32[32,32,128]{2,1,0:T(8,128)} %bitcast.6), calls=%async_computation | async-start | bytes 1048576 | tf_op jit(solution)/shard_map/all_to_all | solution.py:171
  19.4 1.3 %copy-start = (f32[512,1024]{1,0:T(8,128)}, f32[512,1024]{1,0:T(8,128)S(1)}, u32[]{:S(2)}) copy-start(f32[512,1024]{1,0:T(8,128)S(1)} %get-tuple-element.17.scale_ref) | copy-start | bytes 6291460
  20.7 1.0 %copy-start.2 = (bf16[512,1024]{1,0:T(8,128)(2,1)}, bf16[512,1024]{1,0:T(8,128)(2,1)S(1)}, u32[]{:S(2)}) copy-start(bf16[512,1024]{1,0:T(8,128)(2,1)S(1)} %get-tuple-element.15.queries_ref) | copy-start | bytes 3145732
  30.4 1.3 %collective-permute-start = (f32[32,128]{1,0:T(8,128)S(1)}, f32[32,128]{1,0:T(8,128)S(1)}, u32[]{:S(2)}, u32[]{:S(2)}) collective-permute-start(f32[32,128]{1,0:T(8,128)S(1)} %range_total.1), channel_id=1, source_target_pairs={{0,32},{32,0},{64,96},{96,64},{128,160},{160,128},{192,224},{224,1... | collective-permute-start | bytes 49160 | tf_op jit(solution)/shard_map/ppermute | solution.py:189
  31.6 4.9 %collective-permute-start.3 = (f32[32,128]{1,0:T(8,128)S(1)}, f32[32,128]{1,0:T(8,128)S(1)}, u32[]{:S(2)}, u32[]{:S(2)}) collective-permute-start(f32[32,128]{1,0:T(8,128)S(1)} %add.3), channel_id=1, source_target_pairs={{0,192},{32,224},{64,128},{96,160},{128,64},{160,96},{192,0},{224,... | collective-permute-start | bytes 49160 | tf_op jit(solution)/shard_map/ppermute | solution.py:189
  34.6 5.2 %collective-permute-start.2 = (f32[32,128]{1,0:T(8,128)S(1)}, f32[32,128]{1,0:T(8,128)S(1)}, u32[]{:S(2)}, u32[]{:S(2)}) collective-permute-start(f32[32,128]{1,0:T(8,128)S(1)} %add.3), channel_id=1, source_target_pairs={{0,128},{32,160},{64,192},{96,224},{128,0},{160,32},{192,64},{224,... | collective-permute-start | bytes 49160 | tf_op jit(solution)/shard_map/ppermute | solution.py:189
  35.3 4.6 %collective-permute-start.1 = (f32[32,128]{1,0:T(8,128)S(1)}, f32[32,128]{1,0:T(8,128)S(1)}, u32[]{:S(2)}, u32[]{:S(2)}) collective-permute-start(f32[32,128]{1,0:T(8,128)S(1)} %add.3), channel_id=1, source_target_pairs={{0,64},{32,96},{64,0},{96,32},{128,192},{160,224},{192,128},{224,1... | collective-permute-start | bytes 49160 | tf_op jit(solution)/shard_map/ppermute | solution.py:189
  39.9 21.2 %copy-start.1 = (f32[512,1024]{1,0:T(8,128)S(1)}, f32[512,1024]{1,0:T(8,128)}, u32[]{:S(2)}) copy-start(f32[512,1024]{1,0:T(8,128)} %copy-done) | copy-start | bytes 6291460
  39.9 21.2 %copy-start.3 = (bf16[512,1024]{1,0:T(8,128)(2,1)S(1)}, bf16[512,1024]{1,0:T(8,128)(2,1)}, u32[]{:S(2)}) copy-start(bf16[512,1024]{1,0:T(8,128)(2,1)} %copy-done.2) | copy-start | bytes 3145732
